TPU v7x, 768 devices: a whole 4x8x12 slice. The times are simulated.
768 devices in a mesh: ctx: 64 (over x, y, core), exp: 12 (over z).
Axes of the slice: x: 4, y: 8, z: 12, core: 2. Of those that a mesh axis runs over, the one named last changes fastest.
Arguments:
- queries: bfloat16 [8192, 6144], P('ctx', 'exp'), may hold values from -0.71875 to 0.71875
- keys: bfloat16 [8192, 6144], P('ctx', 'exp'), may hold values from -0.71875 to 0.71875
- values: bfloat16 [8192, 6144], P('ctx', 'exp'), may hold values from -0.71875 to 0.71875
- out_grad: bfloat16 [8192, 6144], P('ctx', 'exp'), may hold values from -0.71875 to 0.71875
- log_decay: float32 [8192, 48], P('ctx', 'exp'), may hold values from -1.6 to 0, as said below
- moe_grad: bfloat16 [8192, 6144], P('ctx', 'exp'), may hold values from -6 to 6
- expert_ids: int32 [8192, 2], P('ctx'), may hold values from 0 to 31, all different within a row; in each aligned block of 128 rows (0 to 127, 128 to 255, ...) at most 10 rows name the same one
- gate_weights: float32 [8192, 2], P('ctx'), may hold values from 0.2 to 1
- down_weight: bfloat16 [64, 3072, 6144], P('ctx', 'exp'), may hold values from -0.078125 to 0.078125
Outputs:
- query_grad: bfloat16 [8192, 6144], P('ctx', 'exp')
- key_grad: bfloat16 [8192, 6144], P('ctx', 'exp')
- value_grad: bfloat16 [8192, 6144], P('ctx', 'exp')
- hidden_grad: bfloat16 [64, 640, 3072], P('ctx', None, 'exp')
Inputs may be any that keep to these rules, and one draw needn't show every extreme that they name: `expert_ids`: in the rows of one device (aligned blocks of 128 tokens) no expert is named more than 10 times, and in every draw some expert is named exactly 10 times in some block; a token's two experts differ. `log_decay`: every entry is negative.
All inputs are finite; a program needn't handle non-finite values.
Results may differ from a plain program's by a relative error of at most 0.0049.
Values may be sent and summed in bfloat16 or wider, within the bound.
No kernel may reach another device: no remote copies, remote signals or barrier semaphores. Data moves between devices by JAX's collectives and lax.ppermute only.
A program may use at most 128 MiB of HBM per device.

v0:
```python
import jax
import jax.numpy as jnp
from jax import lax
from jax.sharding import PartitionSpec as P


def carried_in(x, axis, combine, identity, reverse):
    devices, place = (lax.axis_size(axis), lax.axis_index(axis))
    everything = jax.tree.map(lambda part: lax.all_gather(part, axis), x)
    start = jax.tree.map(
        lambda part, zero: jnp.broadcast_to(jnp.asarray(zero, part.dtype), part.shape), x, identity
    )

    def turn(k, before):
        at = devices - 1 - k if reverse else k
        reached = at > place if reverse else at < place
        new = combine(before, jax.tree.map(lambda part: part[at], everything))
        return jax.tree.map(lambda a, b: jnp.where(reached, a, b), new, before)

    return lax.fori_loop(0, devices, turn, start)


def combine_states(earlier, later):
    return (later[1][:, None, None] * earlier[0] + later[0], earlier[1] * later[1])


def attention_grads(queries, keys, values, out_grad, log_decay):
    length, head_count = log_decay.shape
    head_size = queries.shape[1] // head_count
    query_h = queries.reshape(length, head_count, head_size)
    key_h = keys.reshape(length, head_count, head_size)
    value_h = values.reshape(length, head_count, head_size)
    grad_h = out_grad.reshape(length, head_count, head_size)
    running = jnp.cumsum(log_decay, axis=0)
    closing = running[-1]
    causal = jnp.arange(length)[:, None] >= jnp.arange(length)[None, :]
    spread = running.T[:, :, None] - running.T[:, None, :]
    weights = jnp.where(causal[None], jnp.exp(jnp.where(causal[None], spread, 0.0)), 0.0)
    until_finish = jnp.exp(closing[None, :] - running)
    since_beginning = jnp.exp(running)
    query_full = query_h.astype(jnp.float32)
    key_full = key_h.astype(jnp.float32)
    value_full = value_h.astype(jnp.float32)
    gradient_full = grad_h.astype(jnp.float32)
    block_state = jnp.einsum(
        "jqz,jqb->qzb",
        key_full * until_finish[:, :, None],
        value_full,
        precision=lax.Precision.HIGHEST,
    )
    block_grad = jnp.einsum(
        "soj,sop->ojp",
        query_full * since_beginning[:, :, None],
        gradient_full,
        precision=lax.Precision.HIGHEST,
    )
    block_decay = jnp.exp(closing)
    identity_pair = (jnp.zeros_like(block_state), jnp.ones_like(block_decay))
    leading_part, _ = carried_in(
        (block_state, block_decay), "ctx", combine_states, identity_pair, False
    )
    trailing_part, _ = carried_in(
        (block_grad, block_decay), "ctx", combine_states, identity_pair, True
    )
    grad_scores = (
        jnp.einsum("thv,shv->hts", grad_h, value_h, preferred_element_type=jnp.float32) * weights
    ).astype(jnp.bfloat16)
    scores = (
        jnp.einsum("thk,shk->hts", query_h, key_h, preferred_element_type=jnp.float32) * weights
    ).astype(jnp.bfloat16)
    query_grad = jnp.einsum(
        "hts,shk->thk", grad_scores, key_h, preferred_element_type=jnp.float32
    ) + since_beginning[:, :, None] * jnp.einsum(
        "xrq,rgq->xrg", gradient_full, leading_part, precision=lax.Precision.HIGHEST
    )
    key_grad = jnp.einsum(
        "hts,thk->shk", grad_scores, query_h, preferred_element_type=jnp.float32
    ) + until_finish[:, :, None] * jnp.einsum(
        "pox,ofx->pof", value_full, trailing_part, precision=lax.Precision.HIGHEST
    )
    value_grad = jnp.einsum(
        "hts,thv->shv", scores, grad_h, preferred_element_type=jnp.float32
    ) + until_finish[:, :, None] * jnp.einsum(
        "raj,ajb->rab", key_full, trailing_part, precision=lax.Precision.HIGHEST
    )
    flat_width = head_count * head_size
    return (
        query_grad.reshape(length, flat_width).astype(jnp.bfloat16),
        key_grad.reshape(length, flat_width).astype(jnp.bfloat16),
        value_grad.reshape(length, flat_width).astype(jnp.bfloat16),
    )


def route_rows(moe_grad, expert_ids, gate_weights, experts, capacity):
    pair_ids = expert_ids.reshape(-1)
    onehot = (pair_ids[:, None] == jnp.arange(experts)[None, :]).astype(jnp.int32)
    earlier = jnp.cumsum(onehot, axis=0) - onehot
    pair_slots = (pair_ids * capacity + jnp.sum(earlier * onehot, axis=1)).reshape(-1, 2)
    slot_iota = jnp.arange(experts * capacity)[:, None]
    first_table = jnp.where(
        slot_iota == pair_slots[:, 0][None, :], gate_weights[:, 0][None, :], 0.0
    )
    second_table = jnp.where(
        slot_iota == pair_slots[:, 1][None, :], gate_weights[:, 1][None, :], 0.0
    )
    dispatch_table = first_table + second_table
    return jnp.dot(
        dispatch_table, moe_grad.astype(jnp.float32), precision=lax.Precision.HIGHEST
    ).astype(jnp.bfloat16)


def per_device(
    queries, keys, values, out_grad, log_decay, moe_grad, expert_ids, gate_weights, down_weight
):
    query_grad, key_grad, value_grad = attention_grads(queries, keys, values, out_grad, log_decay)
    devices_ctx = lax.axis_size("ctx")
    experts = devices_ctx // 2
    length = moe_grad.shape[0]
    capacity = 5 * length // (2 * experts)
    routed = route_rows(moe_grad, expert_ids, gate_weights, experts, capacity)
    feature_part = routed.shape[1]
    weight_slab = down_weight[0]
    doubled = jnp.broadcast_to(
        routed.reshape(experts, 1, capacity, feature_part), (experts, 2, capacity, feature_part)
    ).reshape(2 * experts * capacity, feature_part)
    arrived = lax.all_to_all(doubled, "ctx", split_axis=0, concat_axis=0, tiled=True)
    hidden = jnp.einsum(
        "sd,fd->sf",
        lax.all_gather(arrived, "exp", axis=1, tiled=True),
        weight_slab,
        preferred_element_type=jnp.float32,
    )
    hidden_grad = hidden.astype(jnp.bfloat16)[None]
    return (query_grad, key_grad, value_grad, hidden_grad)


def solution(mesh):
    in_specs = (
        P("ctx", "exp"),
        P("ctx", "exp"),
        P("ctx", "exp"),
        P("ctx", "exp"),
        P("ctx", "exp"),
        P("ctx", "exp"),
        P("ctx", None),
        P("ctx", None),
        P("ctx", "exp", None),
    )
    out_specs = (P("ctx", "exp"), P("ctx", "exp"), P("ctx", "exp"), P("ctx", None, "exp"))
    return jax.shard_map(
        per_device, mesh=mesh, in_specs=in_specs, out_specs=out_specs, check_vma=False
    )
```

profile of v0, /device:TPU:1, one launch (start us, length us, event | category | flops | bytes accessed | tf_op | source)
XLA Modules:
  0.0 563.6 jit_solution(11723652113854180740)
XLA Ops:
  14.5 43.0 %all_to_all.12 = bf16[64,10,512]{2,1,0:T(8,128)(2,1)} all-to-all(bf16[64,10,512]{2,1,0:T(8,128)(2,1)S(1)} %bitcast.134), channel_id=1, replica_groups=mesh['ctx'=64,'exp'=12] {'ctx'}, dimensions={0} | all-to-all | bytes 1310720 | tf_op jit(solution)/shard_map/all_to_all | solution.py:126
  57.4 2.1 all_to_all.10
  61.1 1.9 fusion.24
  67.3 36.3 %all-gather.2 = f32[64,1,4]{2,1,0:T(1,128)} all-gather(f32[1,1,4]{2,1,0:T(1,128)S(1)} %get-tuple-element.311), channel_id=1, replica_groups=mesh['ctx'=64,'exp'=12] {'ctx'}, dimensions={0}, use_global_device_ids=true | all-gather | bytes 1040 | tf_op jit(solution)/shard_map/all_gather | solution.py:9
  108.1 2.0 convolution_bitcast_fusion.3
  110.2 48.5 %all-gather.7.cloned.1.call-done = bf16[640,6144]{1,0:T(8,128)(2,1)} async-done(((bf16[640,512]{1,0:T(8,128)(2,1)}), bf16[640,6144]{1,0:T(8,128)(2,1)}) %all-gather.7.cloned.1.call-update) | async-done | bytes 7864336 | tf_op jit(solution)/shard_map/all_gather | solution.py:129
  158.7 6.2 %fusion.7 = bf16[1,640,256]{2,1,0:T(8,128)(2,1)} fusion(bf16[640,6144]{1,0:T(8,128)(2,1)} %all-gather.7.cloned.1.call-done, bf16[1,256,6144]{2,1,0:T(8,128)(2,1)S(1)} %copy-done), kind=kOutput, calls=%fused_computation.10 | convolution fusion | flops 2013429760 | bytes 11337728 | tf_op jit(solution)/shard_map/sd,fd->sf/dot_general | solution.py:127
  164.8 106.2 %all-gather.9.cloned.1.call-done = f32[256,128,128]{2,1,0:T(8,128)} async-done(((f32[4,128,128]{2,1,0:T(8,128)}), f32[256,128,128]{2,1,0:T(8,128)}) %all-gather.9.cloned.1.call-update) | async-done | bytes 16777232 | tf_op jit(solution)/shard_map/all_gather | solution.py:9
  271.0 162.2 %while.30 = (s32[]{:T(128)}, f32[4,128,128]{2,1,0:T(8,128)}, s32[]{:T(128)}, f32[64,4]{1,0:T(8,128)}, f32[64,4,128,128]{3,2,1,0:T(8,128)}, /*index=5*/s32[]{:T(128)}, s32[]{:T(128)}) while((s32[]{:T(128)}, f32[4,128,128]{2,1,0:T(8,128)}, s32[]{:T(128)}, f32[64,4]{1,0:T(8,128)}, f32[64,4,128,128]{3,2,1,0:T(8,128)}, ...), condition=%wide.region_2.3_spmd.clone, body=%wide.region_1.2_spmd.clone.sunk | while | flops 262148 | bytes 786593 | solution.py:20
  279.2 1.8 fusion.75
  281.7 1.8 fusion.75
  284.3 1.8 fusion.75
  286.8 1.8 fusion.75
  289.3 1.9 fusion.75
  294.4 1.9 fusion.75
  299.5 1.9 fusion.75
  302.0 1.8 fusion.75
  304.5 1.9 fusion.75
  307.1 1.8 fusion.75
  309.6 1.9 fusion.75
  312.1 1.8 fusion.75
  317.2 1.8 fusion.75
  324.8 1.8 fusion.75
  329.8 1.8 fusion.75
  332.4 1.8 fusion.75
  337.4 1.8 fusion.75
  340.0 1.9 fusion.75
  342.5 2.0 fusion.75
  345.2 1.9 fusion.75
  350.3 1.9 fusion.75
  355.4 1.9 fusion.75
  357.9 1.9 fusion.75
  360.5 1.9 fusion.75
  363.0 1.8 fusion.75
  365.5 1.9 fusion.75
  368.1 1.9 fusion.75
  370.6 1.9 fusion.75
  373.2 1.8 fusion.75
  375.7 1.8 fusion.75
  378.3 1.9 fusion.75
  388.4 1.8 fusion.75
  390.9 1.8 fusion.75
  393.5 1.8 fusion.75
  401.1 1.8 fusion.75
  433.2 2.0 fusion.17
  436.9 112.7 %while.31 = (s32[]{:T(128)}, f32[4,128,128]{2,1,0:T(8,128)S(1)}, s32[]{:T(128)}, f32[64,4]{1,0:T(8,128)}, f32[64,4,128,128]{3,2,1,0:T(8,128)}, /*index=5*/s32[]{:T(128)}, s32[]{:T(128)}, s32[]{:T(128)}, s32[]{:T(128)}) while((s32[]{:T(128)}, f32[4,128,128]{2,1,0:T(8,128)S(1)}, s32[]{:T(128)}, f32[64,4]{1,0:T(8,128)}, ...), condition=%wide.region_4.5_spmd.clone, body=%wide.region_3.4_spmd.clone.sunk | while | flops 262152 | bytes 786655 | solution.py:20
  549.7 2.1 fusion.18
  553.4 2.0 fusion.20
  (277 shorter events, 230.8 us)
Async XLA Ops:
  7.2 151.5 %copy-start = (bf16[1,256,6144]{2,1,0:T(8,128)(2,1)S(1)}, bf16[1,256,6144]{2,1,0:T(8,128)(2,1)}, u32[]{:S(2)}) copy-start(bf16[1,256,6144]{2,1,0:T(8,128)(2,1)} %param.21) | copy-start | bytes 9437188
  7.2 52.4 %copy-start.5 = (f32[128,4]{0,1:T(4,128)S(1)}, f32[128,4]{0,1:T(4,128)}, u32[]{:S(2)}) copy-start(f32[128,4]{0,1:T(4,128)} %param.17) | copy-start | bytes 6148
  7.2 151.5 %all-gather.7.cloned.1.call-start = ((), (), s32[]{:S(2)}) async-start(), calls=%async_computation.1 | async-start | bytes 8519680 | tf_op jit(solution)/shard_map/all_gather | solution.py:129
  59.6 211.4 %all-gather.9.cloned.1.call-start = ((), (), s32[]{:S(2)}) async-start(), calls=%async_computation.2 | async-start | bytes 17039360 | tf_op jit(solution)/shard_map/all_gather | solution.py:9
  60.9 2.0 copy-start.3
  63.0 373.9 %all-gather.11.cloned.1.call-start = ((), (), s32[]{:S(2)}) async-start(), calls=%async_computation.3 | async-start | bytes 17039360 | tf_op jit(solution)/shard_map/all_gather | solution.py:9
  64.1 2.3 copy-start.1
  65.2 1.2 copy-start.2
  103.6 0.6 copy-start.4
Sparse Core Ops, SparseCore 0:
  59.7 98.9 all-gather.6
  162.6 108.3 all-gather.8
  274.9 107.3 all-gather.10
where the time goes:
time: 572 us; the launch traced here: 564 us
  other arithmetic  187 us (33%)
  waiting for transfers between devices  155 us (27%)
  local copies, waits for them, and re-layouts  104 us (18%)
  blocking collectives  79.2 us (14%)
  matrix products  22.6 us (4%)
  between operations  13.9 us (2%)
    select_n x128, other arithmetic, turn(): return jax.tree.map(lambda a, b: jnp.where(reached, a, b), new, before)  186 us
    all_gather x2, waiting for transfers between devices, carried_in(): everything = jax.tree.map(lambda part: lax.all_gather(part, axis), x)  106 us
    mul x128, local copies, waits for them, and re-layouts, combine_states(): later[1][:, None, None] * earlier[0] + later[0]  87.7 us
    all_gather x1, waiting for transfers between devices, per_device(): lax.all_gather(arrived, 'exp', axis=1, tiled=True)  48.5 us
    all_to_all x1, blocking collectives, per_device(): lax.all_to_all(doubled, 'ctx', split_axis=0, concat_axis=0, tiled=True)  43 us
    all_gather x1, blocking collectives, carried_in(): everything = jax.tree.map(lambda part: lax.all_gather(part, axis), x)  36.3 us
  transfers between devices with their start and end apart: 3, of which 2 were waited for; matrix products, arithmetic and copies ran while one was open for 33% of the time, Pallas kernels for 0%

commit v1 on v0

v1 whole, which is shorter than its diff:
```python
import functools

import jax
import jax.numpy as jnp
from jax import lax
from jax.experimental import pallas as pl
from jax.experimental.pallas import tpu as pltpu
from jax.sharding import Mesh, PartitionSpec as P

F32 = jnp.float32
BF16 = jnp.bfloat16
LANES = 128
HEAD = 128
WHOLE = 8
INTERPRET = False


def call(kernel, out_shape, flops, moved, **options):
    return pl.pallas_call(
        kernel,
        out_shape=out_shape,
        interpret=INTERPRET,
        cost_estimate=pl.CostEstimate(flops=flops, bytes_accessed=moved, transcendentals=0),
        **options,
    )


def matmul(a, b):
    return lax.dot_general(a, b, (((1,), (0,)), ((), ())), preferred_element_type=F32)


def matmul_t(a, b):
    return lax.dot_general(a, b, (((1,), (1,)), ((), ())), preferred_element_type=F32)


def pieces(x):
    high = x.astype(BF16)
    rest = x - high.astype(F32)
    middle = rest.astype(BF16)
    return high, middle, (rest - middle.astype(F32)).astype(BF16)


def square(n):
    return (
        lax.broadcasted_iota(jnp.int32, (n, n), 0),
        lax.broadcasted_iota(jnp.int32, (n, n), 1),
    )


def as_row(column, eye):
    return jnp.sum(jnp.where(eye, column, 0.0), axis=0, keepdims=True)


def running_sums(log_decay, row, col):
    lower = jnp.where(row >= col, 1.0, 0.0).astype(BF16)
    high, middle, low = pieces(log_decay)
    return matmul(lower, high) + (matmul(lower, middle) + matmul(lower, low))


def route_kernel(experts, capacity, ids_ref, gate_ref, grad_ref, out_ref):
    length, width = grad_ref.shape
    groups = width // LANES
    tail = capacity - WHOLE
    rows = groups * capacity
    row, col = square(length)
    eye = row == col
    ids = ids_ref[...].astype(F32)
    grad = grad_ref[...].astype(F32)
    names = [as_row(ids[:, j : j + 1], eye) for j in range(2)]
    numbers = lax.broadcasted_iota(jnp.int32, (experts, length), 0).astype(F32)
    chosen = [jnp.where(numbers == name, 1.0, 0.0) for name in names]
    before = jnp.where(row < col, 1.0, 0.0).astype(BF16)
    counts = matmul((chosen[0] + chosen[1]).astype(BF16), before)
    ranks = [jnp.sum(one * counts, axis=0, keepdims=True) for one in chosen]
    scaled = [(gate_ref[:, j : j + 1] * grad).astype(BF16) for j in range(2)]
    chunk = 8
    while experts % chunk:
        chunk //= 2
    for start in range(0, experts, chunk):
        place = lax.broadcasted_iota(jnp.int32, (chunk * rows, 2 * length), 0) + start * rows
        total = None
        for f in range(groups):
            codes = [
                name * rows
                + jnp.where(
                    rank < WHOLE, rank + f * WHOLE, rank + (groups * WHOLE + f * tail - WHOLE)
                )
                for name, rank in zip(names, ranks)
            ]
            code = jnp.concatenate(codes, axis=1).astype(jnp.int32)
            table = jnp.where(place == code, 1.0, 0.0).astype(BF16)
            part = jnp.concatenate([one[:, f * LANES : (f + 1) * LANES] for one in scaled], axis=0)
            product = matmul(table, part)
            total = product if total is None else total + product
        out_ref[start : start + chunk] = total.reshape(chunk, rows, LANES).astype(BF16)


def state_kernel(share, query_ref, key_ref, value_ref, grad_ref, decay_ref, out_ref):
    length, heads = decay_ref.shape
    row, col = square(length)
    eye = row == col
    running = running_sums(decay_ref[...], row, col)
    per_head = HEAD // share
    lines = lax.broadcasted_iota(jnp.int32, (share, LANES), 0)
    for h in range(heads):
        lanes = slice(h * HEAD, (h + 1) * HEAD)
        since = as_row(running[:, h : h + 1], eye)
        closing = running[length - 1 : length, h : h + 1]
        places = slice(h * per_head, (h + 1) * per_head)
        for at, left, right, factor in (
            (0, key_ref, value_ref, jnp.exp(closing - since)),
            (share, query_ref, grad_ref, jnp.exp(since)),
        ):
            turned = left[:, lanes].astype(F32).T * factor
            high = turned.astype(BF16)
            low = (turned - high.astype(F32)).astype(BF16)
            state = matmul(high, right[:, lanes]) + matmul(low, right[:, lanes])
            out_ref[places, at : at + share] = state.astype(BF16).reshape(per_head, share, LANES)
        high, middle, low = [
            part.astype(F32) for part in pieces(jnp.broadcast_to(jnp.exp(closing), (share, LANES)))
        ]
        decay = jnp.where(lines == 0, high, jnp.where(lines == 1, middle, low))
        out_ref[places, 2 * share : 3 * share] = jnp.broadcast_to(
            decay[None], (per_head, share, LANES)
        ).astype(BF16)


def scan_kernel(share, in_ref, out_ref):
    blocks = in_ref.shape[0]

    def step(carried, b, at):
        held = in_ref[b].astype(F32)
        decay = (held[2 * share : 2 * share + 1] + held[2 * share + 1 : 2 * share + 2]) + held[
            2 * share + 2 : 2 * share + 3
        ]
        return carried, decay * carried + held[at : at + share]

    ahead = jnp.zeros((share, LANES), F32)
    behind = jnp.zeros((share, LANES), F32)
    for b in range(blocks):
        now, ahead = step(ahead, b, 0)
        out_ref[b, 0:share] = now
        now, behind = step(behind, blocks - 1 - b, share)
        out_ref[blocks - 1 - b, share : 2 * share] = now


def output_kernel(
    share, query_ref, key_ref, value_ref, grad_ref, decay_ref, carried_ref, dq_ref, dk_ref, dv_ref
):
    length, heads = decay_ref.shape
    row, col = square(length)
    eye = row == col
    running = running_sums(decay_ref[...], row, col)
    per_head = HEAD // share
    for h in range(heads):
        lanes = slice(h * HEAD, (h + 1) * HEAD)
        since = running[:, h : h + 1]
        since_row = as_row(since, eye)
        closing = running[length - 1 : length, h : h + 1]
        carried = carried_ref[h * per_head : (h + 1) * per_head]
        leading = pieces(carried[:, 0:share].reshape(HEAD, LANES))
        trailing = pieces(carried[:, share : 2 * share].reshape(HEAD, LANES))
        q, k, v, g = (ref[:, lanes] for ref in (query_ref, key_ref, value_ref, grad_ref))
        weights = jnp.where(row >= col, jnp.exp(jnp.where(row >= col, since - since_row, 0.0)), 0.0)
        turned = jnp.where(row <= col, jnp.exp(jnp.where(row <= col, since_row - since, 0.0)), 0.0)
        until = jnp.exp(closing - since)
        grad_scores = (matmul_t(g, v) * weights).astype(BF16)
        grad_scores_t = (matmul_t(v, g) * turned).astype(BF16)
        scores_t = (matmul_t(k, q) * turned).astype(BF16)
        dq_ref[:, lanes] = (
            matmul(grad_scores, k) + jnp.exp(since) * (matmul_t(g, leading[0]) + matmul_t(g, leading[1]))
        ).astype(BF16)
        dk_ref[:, lanes] = (
            matmul(grad_scores_t, q)
            + until * (matmul_t(v, trailing[0]) + matmul_t(v, trailing[1]))
        ).astype(BF16)
        dv_ref[:, lanes] = (
            matmul(scores_t, g) + until * (matmul(k, trailing[0]) + matmul(k, trailing[1]))
        ).astype(BF16)


def expert_kernel(capacity, rows_ref, weight_ref, out_ref, total, order):
    step = pl.program_id(0)
    cores, _, sources, lines, _ = rows_ref.shape
    groups = lines // capacity
    tail = capacity - WHOLE
    small = sources * groups * tail
    half = sources * capacity

    @pl.when(step == 0)
    def _():
        row, col = square(small)
        want = (row // tail % sources) * (groups * tail) + (row // (tail * sources)) * tail + row % tail
        order[...] = jnp.where(col == want, 1.0, 0.0).astype(BF16)
        total[...] = jnp.zeros_like(total)

    held = [rows_ref[c, 0] for c in range(cores)]
    rest = [one[:, groups * WHOLE :].reshape(small, LANES) for one in held]
    rest = matmul(order[...], jnp.concatenate(rest, axis=1)).astype(BF16)
    each = small // groups
    left = []
    for c in range(cores):
        whole = [
            held[c][:, f * WHOLE : (f + 1) * WHOLE].reshape(sources * WHOLE, LANES)
            for f in range(groups)
        ]
        left.append(jnp.concatenate(whole, axis=1))
        ends = rest[:, c * LANES : (c + 1) * LANES]
        left.append(jnp.concatenate([ends[f * each : (f + 1) * each] for f in range(groups)], axis=1))
    total[...] += matmul_t(jnp.concatenate(left, axis=0), weight_ref[...])

    @pl.when(step == pl.num_programs(0) - 1)
    def _():
        row, col = square(cores * half)
        block = row // capacity
        slot = row - block * capacity
        source = block // cores
        line = jnp.where(
            slot < WHOLE, source * WHOLE + slot, sources * WHOLE + source * tail + slot - WHOLE
        )
        want = line + (block - source * cores) * half
        place = jnp.where(col == want, 1.0, 0.0).astype(BF16)
        out_ref[0] = matmul(place, total[...].astype(BF16)).astype(BF16)


def per_device(
    queries, keys, values, out_grad, log_decay, moe_grad, expert_ids, gate_weights, down_weight
):
    chips = lax.axis_size("chip")
    blocks = 2 * chips
    experts = chips
    length, width = moe_grad.shape
    capacity = 5 * length // (2 * experts)
    heads = log_decay.shape[1]
    lines = width // LANES * capacity
    share = heads * HEAD // blocks
    weight = down_weight[0]
    hidden = weight.shape[0]

    sent = call(
        functools.partial(route_kernel, experts, capacity),
        jax.ShapeDtypeStruct((experts, lines, LANES), BF16),
        2 * experts * lines * 2 * length * width,
        experts * lines * LANES * 2 + length * width * 2,
        name="route",
    )(expert_ids, gate_weights, moe_grad)
    arrived = lax.all_to_all(sent, "chip", 0, 0, tiled=True)
    gathered = lax.all_gather(arrived, ("core", "exp"), axis=0)

    states = call(
        functools.partial(state_kernel, share),
        jax.ShapeDtypeStruct((blocks, 3 * share, LANES), BF16),
        8 * heads * length * HEAD * HEAD,
        8 * length * width,
        name="states",
    )(queries, keys, values, out_grad, log_decay)
    states, arrived = lax.optimization_barrier((states, arrived))
    spread = lax.all_to_all(states, ("chip", "core"), 0, 0, tiled=True)
    carried = call(
        functools.partial(scan_kernel, share),
        jax.ShapeDtypeStruct((blocks, 2 * share, LANES), F32),
        8 * blocks * share * LANES,
        10 * blocks * share * LANES,
        name="scan",
    )(spread)
    carried = lax.all_to_all(carried, ("chip", "core"), 0, 0, tiled=True)
    flat = jax.ShapeDtypeStruct((length, width), BF16)
    query_grad, key_grad, value_grad = call(
        functools.partial(output_kernel, share),
        (flat, flat, flat),
        18 * heads * length * HEAD * HEAD,
        14 * length * width,
        name="outputs",
    )(queries, keys, values, out_grad, log_decay, carried)

    places = lax.axis_size("exp")
    rows = 2 * chips * capacity
    hidden_grad = call(
        functools.partial(expert_kernel, capacity),
        jax.ShapeDtypeStruct((1, rows, hidden), BF16),
        2 * rows * width * places * hidden,
        2 * (rows + hidden) * width * places,
        grid=(places,),
        in_specs=[
            pl.BlockSpec((2, 1, chips, lines, LANES), lambda z: (0, z, 0, 0, 0)),
            pl.BlockSpec((hidden, width), lambda z: (0, z)),
        ],
        out_specs=pl.BlockSpec((1, rows, hidden), lambda z: (0, 0, 0)),
        scratch_shapes=[
            pltpu.VMEM((rows, hidden), F32),
            pltpu.VMEM(((capacity - WHOLE) * chips * (width // LANES),) * 2, BF16),
        ],
        name="experts",
    )(gathered.reshape(2, places, chips, lines, LANES), weight)
    return (query_grad, key_grad, value_grad, hidden_grad)


def solution(mesh):
    ctx, exp = mesh.devices.shape
    mesh = Mesh(mesh.devices.reshape(ctx // 2, 2, exp), ("chip", "core", "exp"))
    ctx = ("chip", "core")
    in_specs = (
        P(ctx, "exp"),
        P(ctx, "exp"),
        P(ctx, "exp"),
        P(ctx, "exp"),
        P(ctx, "exp"),
        P(ctx, "exp"),
        P(ctx, None),
        P(ctx, None),
        P(ctx, "exp", None),
    )
    out_specs = (P(ctx, "exp"), P(ctx, "exp"), P(ctx, "exp"), P(ctx, None, "exp"))
    return jax.shard_map(
        per_device, mesh=mesh, in_specs=in_specs, out_specs=out_specs, check_vma=False
    )
```

time: 572 us -> 125 us (0.22); the launches traced: 564 us -> 124 us
  other arithmetic: 187 us -> 0 us
  waiting for transfers between devices: 155 us -> 13.9 us
  local copies, waits for them, and re-layouts: 104 us -> 4.25 us
  matrix products: 22.6 us -> 0 us
  Pallas kernels: 0 us -> 22.3 us
  blocking collectives: 79.2 us -> 69.7 us
    select_n x128 -> x0, other arithmetic: 186 us -> none  [turn(): return jax.tree.map(lambda a, b: jnp.where(reached, a, b), new, before)]
    all_gather x3 -> x1, waiting for transfers between devices: 155 us -> 13.9 us  [per_device(): gathered = lax.all_gather(arrived, ('core', 'exp'), axis=0)]
    mul x128 -> x0, local copies, waits for them, and re-layouts: 87.7 us -> none  [combine_states(): later[1][:, None, None] * earlier[0] + later[0]]
    all_gather x1 -> x0, blocking collectives: 36.3 us -> none  [carried_in(): everything = jax.tree.map(lambda part: lax.all_gather(part, axis), x)]
    all_to_all x1 -> x3, blocking collectives: 43 us -> 69.7 us  [the longest x1 25.6 us: per_device(): spread = lax.all_to_all(states, ('chip', 'core'), 0, 0, tiled=True)]
    dot_general x11 -> x0, matrix products: 22.6 us -> none  [the longest x1 6.18 us: per_device(): jnp.einsum('sd,fd->sf', lax.all_gather(arrived, 'exp', axis=1, tiled=True...]
    pallas_call x0 -> x5, Pallas kernels: none -> 22.3 us  [the longest x1 11.7 us: per_device(): call(functools.partial(expert_kernel, capacity), jax.ShapeDtypeStruct((1,...]
  transfers between devices with their start and end apart: 3 -> 1, of which waited for: 2 -> 1; matrix products, arithmetic and copies ran while one was open for 33% -> 1% of each run, Pallas kernels for 0% -> 6%
where the time goes in v1:
time: 125 us; the launch traced here: 124 us
  blocking collectives  69.7 us (56%)
  Pallas kernels  22.3 us (18%)
  between operations  14 us (11%)
  waiting for transfers between devices  13.9 us (11%)
  local copies, waits for them, and re-layouts  4.25 us (3%)
    all_to_all x1, blocking collectives, per_device(): spread = lax.all_to_all(states, ('chip', 'core'), 0, 0, tiled=True)  25.6 us
    all_to_all x1, blocking collectives, per_device(): carried = lax.all_to_all(carried, ('chip', 'core'), 0, 0, tiled=True)  23.6 us
    all_to_all x1, blocking collectives, per_device(): arrived = lax.all_to_all(sent, 'chip', 0, 0, tiled=True)  20.5 us
    all_gather x1, waiting for transfers between devices, per_device(): gathered = lax.all_gather(arrived, ('core', 'exp'), axis=0)  13.9 us
    pallas_call x1, Pallas kernels, per_device(): call(functools.partial(expert_kernel, capacity), jax.ShapeDtypeStruct((1,...  11.7 us
    unnamed x3, local copies, waits for them, and re-layouts  4.25 us
    pallas_call x1, Pallas kernels, per_device(): call(functools.partial(output_kernel, share), (flat, flat, flat), 18 * he...  3.35 us
    pallas_call x1, Pallas kernels, per_device(): call(functools.partial(route_kernel, experts, capacity), jax.ShapeDtypeSt...  2.77 us
  transfers between devices with their start and end apart: 1, of which 1 were waited for; matrix products, arithmetic and copies ran while one was open for 1% of the time, Pallas kernels for 6%

profile of v1, /device:TPU:1, one launch (start us, length us, event | category | flops | bytes accessed | tf_op | source)
XLA Modules:
  0.0 124.2 jit_solution(10534534419292456702)
XLA Ops:
  7.2 0.0 all-gather.3.cloned.1.call-start
  7.2 1.4 %copy.18.ids_ref = s32[128,2]{1,0:T(8,128)} copy(s32[128,2]{0,1:T(2,128)} %param.15) | data formatting | bytes 2048 | tf_op args[6]
  8.6 1.4 %copy.19.gate_ref = f32[128,2]{1,0:T(8,128)} copy(f32[128,2]{0,1:T(2,128)} %param.16) | data formatting | bytes 2048 | tf_op args[7]
  10.0 2.8 %route.1 = bf16[32,40,128]{2,1,0:T(8,128)(2,1)} custom-call(s32[128,2]{1,0:T(8,128)} %copy.18.ids_ref, f32[128,2]{1,0:T(8,128)} %copy.19.gate_ref, bf16[128,512]{1,0:T(8,128)(2,1)} %grad_ref.4), custom_call_target="tpu_custom_call" | custom-call | flops 335544320 | bytes 458752 | tf_op jit(solution)/shard_map/route/pallas_call | solution.py:240
  12.8 20.5 %all_to_all.15 = bf16[32,40,128]{2,1,0:T(8,128)(2,1)} all-to-all(bf16[32,40,128]{2,1,0:T(8,128)(2,1)} %route.1), channel_id=1, replica_groups=mesh['chip'=32,'core'=2,'exp'=12] {'chip'}, dimensions={0} | all-to-all | bytes 655360 | tf_op jit(solution)/shard_map/all_to_all | solution.py:247
  33.3 0.0 all-gather.3.cloned.1.call-update
  33.3 1.4 %copy.20.decay_ref = f32[128,4]{1,0:T(8,128)} copy(f32[128,4]{0,1:T(4,128)} %param.13) | data formatting | bytes 4096 | tf_op args[4]
  34.8 2.5 %states.1 = bf16[64,24,128]{2,1,0:T(8,128)(2,1)} custom-call(bf16[128,512]{1,0:T(8,128)(2,1)} %query_ref.3, bf16[128,512]{1,0:T(8,128)(2,1)} %key_ref.3, bf16[128,512]{1,0:T(8,128)(2,1)} %value_ref.3, bf16[128,512]{1,0:T(8,128)(2,1)} %grad_ref.5, f32[128,4]{1,0:T(8,128)} %copy.20.decay_ref), custom_call_target="tpu_custom_call" | custom-call | flops 67108864 | bytes 524288 | tf_op jit(solution)/shard_map/states/pallas_call | solution.py:250
  37.2 25.6 %all_to_all.16.in_ref = bf16[64,24,128]{2,1,0:T(8,128)(2,1)} all-to-all(bf16[64,24,128]{2,1,0:T(8,128)(2,1)} %states.1), channel_id=1, replica_groups=mesh['chip'=32,'core'=2,'exp'=12] {'chip','core'}, dimensions={0} | all-to-all | bytes 786432 | tf_op jit(solution)/shard_map/all_to_all | solution.py:258
  62.8 2.0 %scan.1 = f32[64,16,128]{2,1,0:T(8,128)} custom-call(bf16[64,24,128]{2,1,0:T(8,128)(2,1)} %all_to_all.16.in_ref), custom_call_target="tpu_custom_call" | custom-call | flops 524288 | bytes 655360 | tf_op jit(solution)/shard_map/scan/pallas_call | solution.py:259
  64.8 23.6 %all_to_all.17.carried_ref = f32[64,16,128]{2,1,0:T(8,128)} all-to-all(f32[64,16,128]{2,1,0:T(8,128)} %scan.1), channel_id=1, replica_groups=mesh['chip'=32,'core'=2,'exp'=12] {'chip','core'}, dimensions={0} | all-to-all | bytes 1048576 | tf_op jit(solution)/shard_map/all_to_all | solution.py:266
  88.4 3.4 %outputs.1 = (bf16[128,512]{1,0:T(8,128)(2,1)}, bf16[128,512]{1,0:T(8,128)(2,1)}, bf16[128,512]{1,0:T(8,128)(2,1)}) custom-call(bf16[128,512]{1,0:T(8,128)(2,1)} %query_ref.3, bf16[128,512]{1,0:T(8,128)(2,1)} %key_ref.3, bf16[128,512]{1,0:T(8,128)(2,1)} %value_ref.3, bf16[128,512]{1,0:T(8,128)(2,1)} %grad_ref.5, f32[128,4]{1,0:T(8,128)} %copy.20.decay_ref, ...), custom_call_target="tpu_custom_call" | custom-call | flops 150994944 | bytes 917504 | tf_op jit(solution)/shard_map/outputs/pallas_call | solution.py:268
  91.7 13.9 %all-gather.3.cloned.1.call-done = bf16[768,40,128]{2,1,0:T(8,128)(2,1)} async-done(((bf16[32,40,128]{2,1,0:T(8,128)(2,1)}), bf16[768,40,128]{2,1,0:T(8,128)(2,1)}) %all-gather.3.cloned.1.call-update) | async-done | bytes 7864336 | tf_op jit(solution)/shard_map/all_gather | solution.py:248
  105.6 11.7 %experts.1 = bf16[1,640,256]{2,1,0:T(8,128)(2,1)} custom-call(bf16[2,12,32,40,128]{4,3,2,1,0:T(8,128)(2,1)} %bitcast.2, bf16[256,6144]{1,0:T(8,128)(2,1)} %bitcast.3), custom_call_target="tpu_custom_call" | custom-call | flops 2013265920 | bytes 11010048 | tf_op jit(solution)/shard_map/experts/pallas_call | solution.py:278
Async XLA Ops:
  7.2 98.5 %all-gather.3.cloned.1.call-start = ((), (), s32[]{:S(2)}) async-start(), calls=%async_computation.3 | async-start | bytes 8192000 | tf_op jit(solution)/shard_map/all_gather | solution.py:248
Sparse Core Ops, SparseCore 0:
  33.5 72.1 all-gather.2

commit v2 on v1

v2 whole, which is shorter than its diff:
```python
import functools

import jax
import jax.numpy as jnp
from jax import lax
from jax.experimental import pallas as pl
from jax.experimental.pallas import tpu as pltpu
from jax.sharding import Mesh, PartitionSpec as P

F32 = jnp.float32
BF16 = jnp.bfloat16
LANES = 128
HEAD = 128
WHOLE = 8
TOGETHER = 4
INTERPRET = False


def call(kernel, out_shape, flops, moved, **options):
    return pl.pallas_call(
        kernel,
        out_shape=out_shape,
        interpret=INTERPRET,
        cost_estimate=pl.CostEstimate(flops=flops, bytes_accessed=moved, transcendentals=0),
        **options,
    )


def matmul(a, b):
    return lax.dot_general(a, b, (((1,), (0,)), ((), ())), preferred_element_type=F32)


def matmul_t(a, b):
    return lax.dot_general(a, b, (((1,), (1,)), ((), ())), preferred_element_type=F32)


def pieces(x):
    high = x.astype(BF16)
    rest = x - high.astype(F32)
    middle = rest.astype(BF16)
    return high, middle, (rest - middle.astype(F32)).astype(BF16)


def square(n):
    return (
        lax.broadcasted_iota(jnp.int32, (n, n), 0),
        lax.broadcasted_iota(jnp.int32, (n, n), 1),
    )


def as_column(line, eye):
    return jnp.sum(jnp.where(eye, line, 0.0), axis=1, keepdims=True)


def running_sums(log_decay, row, col):
    upper = jnp.where(row <= col, 1.0, 0.0).astype(BF16)
    high, middle, low = pieces(log_decay)
    return matmul(high, upper) + (matmul(middle, upper) + matmul(low, upper))


def one_hot(want, columns):
    places = lax.broadcasted_iota(jnp.int32, (want.shape[0], columns), 1)
    return jnp.where(places == want, 1.0, 0.0).astype(BF16)


def counting(n):
    return lax.broadcasted_iota(jnp.int32, (n, 1), 0)


def route_kernel(experts, capacity, ids_ref, gate_ref, grad_ref, out_ref):
    length, width = grad_ref.shape
    groups = width // LANES
    tail = capacity - WHOLE
    most = experts * WHOLE
    row, col = square(length)
    eye = row == col
    ids = ids_ref[...].astype(F32)
    grad = grad_ref[...].astype(F32)
    names = [ids[j : j + 1] for j in range(2)]
    numbers = lax.broadcasted_iota(jnp.int32, (experts, length), 0).astype(F32)
    chosen = [jnp.where(numbers == name, 1.0, 0.0) for name in names]
    before = jnp.where(row < col, 1.0, 0.0).astype(BF16)
    counts = matmul((chosen[0] + chosen[1]).astype(BF16), before)
    ranks = [jnp.sum(one * counts, axis=0, keepdims=True) for one in chosen]
    scaled = [(as_column(gate_ref[j : j + 1], eye) * grad).astype(BF16) for j in range(2)]
    codes = [
        jnp.where(rank < WHOLE, name * WHOLE + rank, name * tail + rank + (most - WHOLE))
        for name, rank in zip(names, ranks)
    ]
    code = jnp.concatenate(codes, axis=1).astype(jnp.int32)
    place = lax.broadcasted_iota(jnp.int32, (experts * capacity, 2 * length), 0)
    table = jnp.where(place == code, 1.0, 0.0).astype(BF16)
    routed = matmul(table, jnp.concatenate(scaled, axis=0)).astype(BF16)
    parts = [routed[:, f * LANES : (f + 1) * LANES] for f in range(groups)]
    for f in range(groups):
        out_ref[:, f * WHOLE : (f + 1) * WHOLE] = parts[f][:most].reshape(experts, WHOLE, LANES)
    rest = jnp.concatenate([part[most:] for part in parts], axis=0)
    line = counting(experts * groups * tail)
    expert = line // (groups * tail)
    f = (line - expert * (groups * tail)) // tail
    want = f * (experts * tail) + expert * tail + (line - expert * (groups * tail) - f * tail)
    rest = matmul(one_hot(want, experts * groups * tail), rest).astype(BF16)
    out_ref[:, groups * WHOLE :] = rest.reshape(experts, groups * tail, LANES)


def state_kernel(share, query_ref, key_ref, value_ref, grad_ref, decay_ref, out_ref):
    heads, length = decay_ref.shape
    row, col = square(length)
    running = running_sums(decay_ref[...], row, col)
    per_head = HEAD // share
    lines = lax.broadcasted_iota(jnp.int32, (share, LANES), 0)
    for h in range(heads):
        lanes = slice(h * HEAD, (h + 1) * HEAD)
        since = running[h : h + 1]
        closing = running[h : h + 1, length - 1 : length]
        places = slice(h * per_head, (h + 1) * per_head)
        for at, left, right, factor in (
            (0, key_ref, value_ref, jnp.exp(closing - since)),
            (share, query_ref, grad_ref, jnp.exp(since)),
        ):
            turned = left[:, lanes].astype(F32).T * factor
            high = turned.astype(BF16)
            low = (turned - high.astype(F32)).astype(BF16)
            state = matmul(high, right[:, lanes]) + matmul(low, right[:, lanes])
            out_ref[places, at : at + share] = state.astype(BF16).reshape(per_head, share, LANES)
        high, middle, low = [
            part.astype(F32) for part in pieces(jnp.broadcast_to(jnp.exp(closing), (share, LANES)))
        ]
        decay = jnp.where(lines == 0, high, jnp.where(lines == 1, middle, low))
        out_ref[places, 2 * share : 3 * share] = jnp.broadcast_to(
            decay[None], (per_head, share, LANES)
        ).astype(BF16)


def scan_kernel(share, in_ref, out_ref):
    blocks = in_ref.shape[0]

    def step(carried, b, at):
        held = in_ref[b].astype(F32)
        decay = (held[2 * share : 2 * share + 1] + held[2 * share + 1 : 2 * share + 2]) + held[
            2 * share + 2 : 2 * share + 3
        ]
        return carried, decay * carried + held[at : at + share]

    ahead = jnp.zeros((share, LANES), F32)
    behind = jnp.zeros((share, LANES), F32)
    for b in range(blocks):
        now, ahead = step(ahead, b, 0)
        out_ref[b, 0:share] = now.astype(BF16)
        now, behind = step(behind, blocks - 1 - b, share)
        out_ref[blocks - 1 - b, share : 2 * share] = now.astype(BF16)


def output_kernel(
    share, query_ref, key_ref, value_ref, grad_ref, decay_ref, carried_ref, dq_ref, dk_ref, dv_ref
):
    heads, length = decay_ref.shape
    row, col = square(length)
    eye = row == col
    running = running_sums(decay_ref[...], row, col)
    per_head = HEAD // share
    for h in range(heads):
        lanes = slice(h * HEAD, (h + 1) * HEAD)
        since_row = running[h : h + 1]
        since = as_column(since_row, eye)
        closing = since_row[:, length - 1 : length]
        carried = carried_ref[h * per_head : (h + 1) * per_head]
        leading = carried[:, 0:share].reshape(HEAD, LANES)
        trailing = carried[:, share : 2 * share].reshape(HEAD, LANES)
        q, k, v, g = (ref[:, lanes] for ref in (query_ref, key_ref, value_ref, grad_ref))
        weights = jnp.where(row >= col, jnp.exp(jnp.where(row >= col, since - since_row, 0.0)), 0.0)
        turned = jnp.where(row <= col, jnp.exp(jnp.where(row <= col, since_row - since, 0.0)), 0.0)
        until = jnp.exp(closing - since)
        grad_scores = (matmul_t(g, v) * weights).astype(BF16)
        grad_scores_t = (matmul_t(v, g) * turned).astype(BF16)
        scores_t = (matmul_t(k, q) * turned).astype(BF16)
        dq_ref[:, lanes] = (
            matmul(grad_scores, k) + jnp.exp(since) * matmul_t(g, leading)
        ).astype(BF16)
        dk_ref[:, lanes] = (
            matmul(grad_scores_t, q)
            + until * matmul_t(v, trailing)
        ).astype(BF16)
        dv_ref[:, lanes] = (
            matmul(scores_t, g) + until * matmul(k, trailing)
        ).astype(BF16)


def expert_kernel(capacity, rows_ref, weight_ref, out_ref, total, order):
    step = pl.program_id(0)
    cores, places, sources, lines, _ = rows_ref.shape
    groups = lines // capacity
    tail = capacity - WHOLE
    small = sources * groups * tail
    half = sources * capacity

    @pl.when(step == 0)
    def _():
        row = counting(small)
        f = row // (tail * sources)
        source = (row - f * (tail * sources)) // tail
        slot = row - f * (tail * sources) - source * tail
        order[...] = one_hot(source * (groups * tail) + f * tail + slot, small)

    held = [[rows_ref[c, z] for z in range(places)] for c in range(cores)]
    rest = [one[:, groups * WHOLE :].reshape(small, LANES) for each in held for one in each]
    rest = matmul(order[...], jnp.concatenate(rest, axis=1)).astype(BF16)
    each = small // groups
    left = []
    for c in range(cores):
        whole = [
            held[c][z][:, f * WHOLE : (f + 1) * WHOLE].reshape(sources * WHOLE, LANES)
            for z in range(places)
            for f in range(groups)
        ]
        left.append(jnp.concatenate(whole, axis=1))
        ends = rest[:, c * places * LANES : (c + 1) * places * LANES]
        ends = [
            ends[f * each : (f + 1) * each, z * LANES : (z + 1) * LANES]
            for z in range(places)
            for f in range(groups)
        ]
        left.append(jnp.concatenate(ends, axis=1))
    product = matmul_t(jnp.concatenate(left, axis=0), weight_ref[...])

    @pl.when(step == 0)
    def _():
        total[...] = product

    @pl.when(step > 0)
    def _():
        total[...] += product

    @pl.when(step == pl.num_programs(0) - 1)
    def _():
        lot = WHOLE // tail
        size = cores * lot * capacity
        row = counting(size)
        block = row // capacity
        slot = row - block * capacity
        source = block // cores
        line = jnp.where(slot < WHOLE, source * WHOLE + slot, lot * WHOLE + source * tail + slot - WHOLE)
        place = one_hot(line + (block - source * cores) * (lot * capacity), size)
        for g in range(sources // lot):
            taken = []
            for c in range(cores):
                first = c * half + g * lot * WHOLE
                taken.append(total[first : first + lot * WHOLE])
                first = c * half + sources * WHOLE + g * lot * tail
                taken.append(total[first : first + lot * tail])
            taken = jnp.concatenate(taken, axis=0).astype(BF16)
            out_ref[0, g * size : (g + 1) * size] = matmul(place, taken).astype(BF16)


def per_device(
    queries, keys, values, out_grad, log_decay, moe_grad, expert_ids, gate_weights, down_weight
):
    chips = lax.axis_size("chip")
    blocks = 2 * chips
    experts = chips
    length, width = moe_grad.shape
    decay = log_decay.T
    capacity = 5 * length // (2 * experts)
    heads = log_decay.shape[1]
    lines = width // LANES * capacity
    share = heads * HEAD // blocks
    weight = down_weight[0]
    hidden = weight.shape[0]

    sent = call(
        functools.partial(route_kernel, experts, capacity),
        jax.ShapeDtypeStruct((experts, lines, LANES), BF16),
        2 * experts * lines * 2 * length * width,
        experts * lines * LANES * 2 + length * width * 2,
        name="route",
    )(expert_ids.T, gate_weights.T, moe_grad)
    arrived = lax.all_to_all(sent, "chip", 0, 0, tiled=True)
    gathered = lax.all_gather(arrived, ("core", "exp"), axis=0)

    states = call(
        functools.partial(state_kernel, share),
        jax.ShapeDtypeStruct((blocks, 3 * share, LANES), BF16),
        8 * heads * length * HEAD * HEAD,
        8 * length * width,
        name="states",
    )(queries, keys, values, out_grad, decay)
    states, arrived = lax.optimization_barrier((states, arrived))
    spread = lax.all_to_all(states, ("chip", "core"), 0, 0, tiled=True)
    carried = call(
        functools.partial(scan_kernel, share),
        jax.ShapeDtypeStruct((blocks, 2 * share, LANES), BF16),
        8 * blocks * share * LANES,
        10 * blocks * share * LANES,
        name="scan",
    )(spread)
    carried = lax.all_to_all(carried, ("chip", "core"), 0, 0, tiled=True)
    flat = jax.ShapeDtypeStruct((length, width), BF16)
    query_grad, key_grad, value_grad = call(
        functools.partial(output_kernel, share),
        (flat, flat, flat),
        18 * heads * length * HEAD * HEAD,
        14 * length * width,
        name="outputs",
    )(queries, keys, values, out_grad, decay, carried)

    places = lax.axis_size("exp")
    rows = 2 * chips * capacity
    deep = TOGETHER if places % TOGETHER == 0 else 1
    hidden_grad = call(
        functools.partial(expert_kernel, capacity),
        jax.ShapeDtypeStruct((1, rows, hidden), BF16),
        2 * rows * width * places * hidden,
        2 * (rows + hidden) * width * places,
        grid=(places // deep,),
        in_specs=[
            pl.BlockSpec((2, deep, chips, lines, LANES), lambda z: (0, z, 0, 0, 0)),
            pl.BlockSpec((hidden, deep * width), lambda z: (0, z)),
        ],
        out_specs=pl.BlockSpec((1, rows, hidden), lambda z: (0, 0, 0)),
        scratch_shapes=[
            pltpu.VMEM((rows, hidden), F32),
            pltpu.VMEM(((capacity - WHOLE) * chips * (width // LANES),) * 2, BF16),
        ],
        name="experts",
    )(gathered.reshape(2, places, chips, lines, LANES), weight)
    return (query_grad, key_grad, value_grad, hidden_grad)


def solution(mesh):
    ctx, exp = mesh.devices.shape
    mesh = Mesh(mesh.devices.reshape(ctx // 2, 2, exp), ("chip", "core", "exp"))
    ctx = ("chip", "core")
    in_specs = (
        P(ctx, "exp"),
        P(ctx, "exp"),
        P(ctx, "exp"),
        P(ctx, "exp"),
        P(ctx, "exp"),
        P(ctx, "exp"),
        P(ctx, None),
        P(ctx, None),
        P(ctx, "exp", None),
    )
    out_specs = (P(ctx, "exp"), P(ctx, "exp"), P(ctx, "exp"), P(ctx, None, "exp"))
    return jax.shard_map(
        per_device, mesh=mesh, in_specs=in_specs, out_specs=out_specs, check_vma=False
    )
```

time: 125 us -> 117 us (0.936)
  waiting for transfers between devices: 13.9 us -> 21.1 us
  Pallas kernels: 22.3 us -> 16.8 us
  blocking collectives: 69.7 us -> 64.4 us
  local copies, waits for them, and re-layouts: 4.25 us -> 0 us
    all_gather x1, waiting for transfers between devices: 13.9 us -> 21.1 us  [per_device(): gathered = lax.all_gather(arrived, ('core', 'exp'), axis=0)]
    all_to_all x1, blocking collectives: 23.6 us -> 18.3 us  [per_device(): carried = lax.all_to_all(carried, ('chip', 'core'), 0, 0, tiled=True)]
    pallas_call x1, Pallas kernels: 11.7 us -> 7.23 us  [per_device(): call(functools.partial(expert_kernel, capacity), jax.ShapeDtypeStruct((1,...]
    unnamed x3 -> x0, local copies, waits for them, and re-layouts: 4.25 us -> none
  transfers between devices with their start and end apart: 1 -> 1, of which waited for: 1 -> 1; matrix products, arithmetic and copies ran while one was open for 1% -> 0% of each run, Pallas kernels for 6% -> 6%
where the time goes in v2:
time: 117 us; the launch traced here: 116 us
  blocking collectives  64.4 us (55%)
  waiting for transfers between devices  21.1 us (18%)
  Pallas kernels  16.8 us (14%)
  between operations  14 us (12%)
    all_to_all x1, blocking collectives, per_device(): spread = lax.all_to_all(states, ('chip', 'core'), 0, 0, tiled=True)  25.6 us
    all_gather x1, waiting for transfers between devices, per_device(): gathered = lax.all_gather(arrived, ('core', 'exp'), axis=0)  21.1 us
    all_to_all x1, blocking collectives, per_device(): arrived = lax.all_to_all(sent, 'chip', 0, 0, tiled=True)  20.5 us
    all_to_all x1, blocking collectives, per_device(): carried = lax.all_to_all(carried, ('chip', 'core'), 0, 0, tiled=True)  18.3 us
    pallas_call x1, Pallas kernels, per_device(): call(functools.partial(expert_kernel, capacity), jax.ShapeDtypeStruct((1,...  7.23 us
    pallas_call x1, Pallas kernels, per_device(): call(functools.partial(output_kernel, share), (flat, flat, flat), 18 * he...  3 us
    pallas_call x1, Pallas kernels, per_device(): call(functools.partial(state_kernel, share), jax.ShapeDtypeStruct((blocks...  2.42 us
  transfers between devices with their start and end apart: 1, of which 1 were waited for; matrix products, arithmetic and copies ran while one was open for 0% of the time, Pallas kernels for 6%

profile of v2, /device:TPU:1, one launch (start us, length us, event | category | flops | bytes accessed | tf_op | source)
XLA Modules:
  0.0 116.3 jit_solution(551526084512836850)
XLA Ops:
  7.2 0.0 all-gather.3.cloned.1.call-start
  7.2 2.2 %route.1 = bf16[32,40,128]{2,1,0:T(8,128)(2,1)} custom-call(s32[2,128]{1,0:T(2,128)} %bitcast.9, f32[2,128]{1,0:T(2,128)} %bitcast.10, bf16[128,512]{1,0:T(8,128)(2,1)} %grad_ref.4), custom_call_target="tpu_custom_call" | custom-call | flops 335544320 | bytes 458752 | tf_op jit(solution)/shard_map/route/pallas_call | solution.py:270
  9.5 20.5 %all_to_all.15 = bf16[32,40,128]{2,1,0:T(8,128)(2,1)} all-to-all(bf16[32,40,128]{2,1,0:T(8,128)(2,1)} %route.1), channel_id=1, replica_groups=mesh['chip'=32,'core'=2,'exp'=12] {'chip'}, dimensions={0} | all-to-all | bytes 655360 | tf_op jit(solution)/shard_map/all_to_all | solution.py:277
  30.0 0.0 all-gather.3.cloned.1.call-update
  30.0 2.4 %states.1 = bf16[64,24,128]{2,1,0:T(8,128)(2,1)} custom-call(bf16[128,512]{1,0:T(8,128)(2,1)} %query_ref.3, bf16[128,512]{1,0:T(8,128)(2,1)} %key_ref.3, bf16[128,512]{1,0:T(8,128)(2,1)} %value_ref.3, bf16[128,512]{1,0:T(8,128)(2,1)} %grad_ref.5, f32[4,128]{1,0:T(4,128)} %bitcast.7), custom_call_target="tpu_custom_call" | custom-call | flops 67108864 | bytes 524288 | tf_op jit(solution)/shard_map/states/pallas_call | solution.py:280
  32.4 25.6 %all_to_all.16.in_ref = bf16[64,24,128]{2,1,0:T(8,128)(2,1)} all-to-all(bf16[64,24,128]{2,1,0:T(8,128)(2,1)} %states.1), channel_id=1, replica_groups=mesh['chip'=32,'core'=2,'exp'=12] {'chip','core'}, dimensions={0} | all-to-all | bytes 786432 | tf_op jit(solution)/shard_map/all_to_all | solution.py:288
  58.0 1.9 %scan.1 = bf16[64,16,128]{2,1,0:T(8,128)(2,1)} custom-call(bf16[64,24,128]{2,1,0:T(8,128)(2,1)} %all_to_all.16.in_ref), custom_call_target="tpu_custom_call" | custom-call | flops 524288 | bytes 655360 | tf_op jit(solution)/shard_map/scan/pallas_call | solution.py:289
  59.8 18.3 %all_to_all.17.carried_ref = bf16[64,16,128]{2,1,0:T(8,128)(2,1)} all-to-all(bf16[64,16,128]{2,1,0:T(8,128)(2,1)} %scan.1), channel_id=1, replica_groups=mesh['chip'=32,'core'=2,'exp'=12] {'chip','core'}, dimensions={0} | all-to-all | bytes 524288 | tf_op jit(solution)/shard_map/all_to_all | solution.py:296
  78.1 3.0 %outputs.1 = (bf16[128,512]{1,0:T(8,128)(2,1)}, bf16[128,512]{1,0:T(8,128)(2,1)}, bf16[128,512]{1,0:T(8,128)(2,1)}) custom-call(bf16[128,512]{1,0:T(8,128)(2,1)} %query_ref.3, bf16[128,512]{1,0:T(8,128)(2,1)} %key_ref.3, bf16[128,512]{1,0:T(8,128)(2,1)} %value_ref.3, bf16[128,512]{1,0:T(8,128)(2,1)} %grad_ref.5, f32[4,128]{1,0:T(4,128)} %bitcast.8, ...), custom_call_target="tpu_custom_call" | custom-call | flops 150994944 | bytes 917504 | tf_op jit(solution)/shard_map/outputs/pallas_call | solution.py:298
  81.1 21.1 %all-gather.3.cloned.1.call-done = bf16[768,40,128]{2,1,0:T(8,128)(2,1)} async-done(((bf16[32,40,128]{2,1,0:T(8,128)(2,1)}), bf16[768,40,128]{2,1,0:T(8,128)(2,1)}) %all-gather.3.cloned.1.call-update) | async-done | bytes 7864336 | tf_op jit(solution)/shard_map/all_gather | solution.py:278
  102.3 7.2 %experts.1 = bf16[1,640,256]{2,1,0:T(8,128)(2,1)} custom-call(bf16[2,12,32,40,128]{4,3,2,1,0:T(8,128)(2,1)} %bitcast.5, bf16[256,6144]{1,0:T(8,128)(2,1)} %bitcast.6), custom_call_target="tpu_custom_call" | custom-call | flops 2013265920 | bytes 11010048 | tf_op jit(solution)/shard_map/experts/pallas_call | solution.py:309
Async XLA Ops:
  7.2 95.1 %all-gather.3.cloned.1.call-start = ((), (), s32[]{:S(2)}) async-start(), calls=%async_computation.3 | async-start | bytes 8192000 | tf_op jit(solution)/shard_map/all_gather | solution.py:278
Sparse Core Ops, SparseCore 0:
  30.1 72.1 all-gather.2

commit v3 on v2

--- a/solution.py
+++ b/solution.py
@@ -24,6 +24,10 @@
         cost_estimate=pl.CostEstimate(flops=flops, bytes_accessed=moved, transcendentals=0),
         **options,
     )
+
+
+def in_hbm(x):
+    return x if INTERPRET else pltpu.with_memory_space_constraint(x, pltpu.HBM)
 
 
 def matmul(a, b):
@@ -151,9 +155,41 @@
         out_ref[blocks - 1 - b, share : 2 * share] = now.astype(BF16)
 
 
+def fill_tables(capacity, sources, groups, order_ref, place_ref):
+    tail = capacity - WHOLE
+    small = sources * groups * tail
+    row = counting(small)
+    f = row // (tail * sources)
+    source = (row - f * (tail * sources)) // tail
+    slot = row - f * (tail * sources) - source * tail
+    order_ref[...] = one_hot(source * (groups * tail) + f * tail + slot, small)
+    lot = WHOLE // tail
+    size = 2 * lot * capacity
+    row = counting(size)
+    block = row // capacity
+    slot = row - block * capacity
+    source = block // 2
+    line = jnp.where(slot < WHOLE, source * WHOLE + slot, lot * WHOLE + source * tail + slot - WHOLE)
+    place_ref[...] = one_hot(line + (block - source * 2) * (lot * capacity), size)
+
+
 def output_kernel(
-    share, query_ref, key_ref, value_ref, grad_ref, decay_ref, carried_ref, dq_ref, dk_ref, dv_ref
+    share,
+    capacity,
+    sources,
+    query_ref,
+    key_ref,
+    value_ref,
+    grad_ref,
+    decay_ref,
+    carried_ref,
+    dq_ref,
+    dk_ref,
+    dv_ref,
+    order_ref,
+    place_ref,
 ):
+    fill_tables(capacity, sources, query_ref.shape[1] // LANES, order_ref, place_ref)
     heads, length = decay_ref.shape
     row, col = square(length)
     eye = row == col
@@ -186,7 +222,7 @@
         ).astype(BF16)
 
 
-def expert_kernel(capacity, rows_ref, weight_ref, out_ref, total, order):
+def expert_kernel(capacity, rows_ref, weight_ref, order_ref, place_ref, out_ref, total):
     step = pl.program_id(0)
     cores, places, sources, lines, _ = rows_ref.shape
     groups = lines // capacity
@@ -194,17 +230,9 @@
     small = sources * groups * tail
     half = sources * capacity
 
-    @pl.when(step == 0)
-    def _():
-        row = counting(small)
-        f = row // (tail * sources)
-        source = (row - f * (tail * sources)) // tail
-        slot = row - f * (tail * sources) - source * tail
-        order[...] = one_hot(source * (groups * tail) + f * tail + slot, small)
-
     held = [[rows_ref[c, z] for z in range(places)] for c in range(cores)]
     rest = [one[:, groups * WHOLE :].reshape(small, LANES) for each in held for one in each]
-    rest = matmul(order[...], jnp.concatenate(rest, axis=1)).astype(BF16)
+    rest = matmul(order_ref[...], jnp.concatenate(rest, axis=1)).astype(BF16)
     each = small // groups
     left = []
     for c in range(cores):
@@ -235,12 +263,6 @@
     def _():
         lot = WHOLE // tail
         size = cores * lot * capacity
-        row = counting(size)
-        block = row // capacity
-        slot = row - block * capacity
-        source = block // cores
-        line = jnp.where(slot < WHOLE, source * WHOLE + slot, lot * WHOLE + source * tail + slot - WHOLE)
-        place = one_hot(line + (block - source * cores) * (lot * capacity), size)
         for g in range(sources // lot):
             taken = []
             for c in range(cores):
@@ -249,7 +271,7 @@
                 first = c * half + sources * WHOLE + g * lot * tail
                 taken.append(total[first : first + lot * tail])
             taken = jnp.concatenate(taken, axis=0).astype(BF16)
-            out_ref[0, g * size : (g + 1) * size] = matmul(place, taken).astype(BF16)
+            out_ref[0, g * size : (g + 1) * size] = matmul(place_ref[...], taken).astype(BF16)
 
 
 def per_device(
@@ -272,8 +294,9 @@
         jax.ShapeDtypeStruct((experts, lines, LANES), BF16),
         2 * experts * lines * 2 * length * width,
         experts * lines * LANES * 2 + length * width * 2,
+        compiler_params=pltpu.CompilerParams(vmem_limit_bytes=16 << 20),
         name="route",
-    )(expert_ids.T, gate_weights.T, moe_grad)
+    )(in_hbm(expert_ids.T), in_hbm(gate_weights.T), in_hbm(moe_grad))
     arrived = lax.all_to_all(sent, "chip", 0, 0, tiled=True)
     gathered = lax.all_gather(arrived, ("core", "exp"), axis=0)
 
@@ -294,10 +317,19 @@
         name="scan",
     )(spread)
     carried = lax.all_to_all(carried, ("chip", "core"), 0, 0, tiled=True)
+    weight, carried = lax.optimization_barrier((weight, carried))
     flat = jax.ShapeDtypeStruct((length, width), BF16)
-    query_grad, key_grad, value_grad = call(
-        functools.partial(output_kernel, share),
-        (flat, flat, flat),
+    small = (capacity - WHOLE) * chips * (width // LANES)
+    size = 2 * capacity * (WHOLE // (capacity - WHOLE))
+    query_grad, key_grad, value_grad, order, place = call(
+        functools.partial(output_kernel, share, capacity, chips),
+        (
+            flat,
+            flat,
+            flat,
+            jax.ShapeDtypeStruct((small, small), BF16),
+            jax.ShapeDtypeStruct((size, size), BF16),
+        ),
         18 * heads * length * HEAD * HEAD,
         14 * length * width,
         name="outputs",
@@ -312,17 +344,19 @@
         2 * rows * width * places * hidden,
         2 * (rows + hidden) * width * places,
         grid=(places // deep,),
+        compiler_params=pltpu.CompilerParams(vmem_limit_bytes=24 << 20),
         in_specs=[
             pl.BlockSpec((2, deep, chips, lines, LANES), lambda z: (0, z, 0, 0, 0)),
             pl.BlockSpec((hidden, deep * width), lambda z: (0, z)),
+            pl.BlockSpec((small, small), lambda z: (0, 0)),
+            pl.BlockSpec((size, size), lambda z: (0, 0)),
         ],
         out_specs=pl.BlockSpec((1, rows, hidden), lambda z: (0, 0, 0)),
         scratch_shapes=[
             pltpu.VMEM((rows, hidden), F32),
-            pltpu.VMEM(((capacity - WHOLE) * chips * (width // LANES),) * 2, BF16),
         ],
         name="experts",
-    )(gathered.reshape(2, places, chips, lines, LANES), weight)
+    )(in_hbm(gathered.reshape(2, places, chips, lines, LANES)), weight, order, place)
     return (query_grad, key_grad, value_grad, hidden_grad)
 
 

time: 117 us -> 117 us (level)
  local copies, waits for them, and re-layouts: 0 us -> 1.64 us
  Pallas kernels: 16.8 us -> 15.6 us
    unnamed x0 -> x6, local copies, waits for them, and re-layouts: none -> 1.64 us
where the time goes in v3:
time: 117 us; the launch traced here: 116 us
  blocking collectives  63.5 us (54%)
  waiting for transfers between devices  21.7 us (19%)
  Pallas kernels  15.6 us (13%)
  between operations  14 us (12%)
  local copies, waits for them, and re-layouts  1.64 us (1%)
    all_to_all x1, blocking collectives, per_device(): spread = lax.all_to_all(states, ('chip', 'core'), 0, 0, tiled=True)  24.8 us
    all_gather x1, waiting for transfers between devices, per_device(): gathered = lax.all_gather(arrived, ('core', 'exp'), axis=0)  21.6 us
    all_to_all x1, blocking collectives, per_device(): arrived = lax.all_to_all(sent, 'chip', 0, 0, tiled=True)  20.4 us
    all_to_all x1, blocking collectives, per_device(): carried = lax.all_to_all(carried, ('chip', 'core'), 0, 0, tiled=True)  18.3 us
    pallas_call x1, Pallas kernels, per_device(): call(functools.partial(expert_kernel, capacity), jax.ShapeDtypeStruct((1,...  6.5 us
    pallas_call x1, Pallas kernels, per_device(): call(functools.partial(output_kernel, share, capacity, chips), (flat, fla...  3.16 us
    pallas_call x1, Pallas kernels, per_device(): call(functools.partial(state_kernel, share), jax.ShapeDtypeStruct((blocks...  2.44 us
  transfers between devices with their start and end apart: 1, of which 1 were waited for; matrix products, arithmetic and copies ran while one was open for 0% of the time, Pallas kernels for 6%

profile of v3, /device:TPU:1, one launch (start us, length us, event | category | flops | bytes accessed | tf_op | source)
XLA Modules:
  0.0 116.5 jit_solution(17009628804983923304)
XLA Ops:
  7.2 0.0 copy-start
  7.2 0.0 all-gather.3.cloned.1.call-start
  7.2 1.7 %route.1 = bf16[32,40,128]{2,1,0:T(8,128)(2,1)S(1)} custom-call(s32[2,128]{1,0:T(2,128)} %bitcast.9, f32[2,128]{1,0:T(2,128)} %bitcast.10, bf16[128,512]{1,0:T(8,128)(2,1)} %grad_ref.4), custom_call_target="tpu_custom_call" | custom-call | flops 335544320 | bytes 458752 | tf_op jit(solution)/shard_map/route/pallas_call | solution.py:292
  8.9 20.4 %all_to_all.15 = bf16[32,40,128]{2,1,0:T(8,128)(2,1)} all-to-all(bf16[32,40,128]{2,1,0:T(8,128)(2,1)S(1)} %route.1), channel_id=1, replica_groups=mesh['chip'=32,'core'=2,'exp'=12] {'chip'}, dimensions={0} | all-to-all | bytes 655360 | tf_op jit(solution)/shard_map/all_to_all | solution.py:300
  29.3 0.0 all-gather.3.cloned.1.call-update
  29.3 2.4 %states.1 = bf16[64,24,128]{2,1,0:T(8,128)(2,1)} custom-call(bf16[128,512]{1,0:T(8,128)(2,1)} %query_ref.3, bf16[128,512]{1,0:T(8,128)(2,1)} %key_ref.3, bf16[128,512]{1,0:T(8,128)(2,1)} %value_ref.3, bf16[128,512]{1,0:T(8,128)(2,1)} %grad_ref.5, f32[4,128]{1,0:T(4,128)} %bitcast.7), custom_call_target="tpu_custom_call" | custom-call | flops 67108864 | bytes 524288 | tf_op jit(solution)/shard_map/states/pallas_call | solution.py:303
  31.8 24.8 %all_to_all.16.in_ref = bf16[64,24,128]{2,1,0:T(8,128)(2,1)} all-to-all(bf16[64,24,128]{2,1,0:T(8,128)(2,1)} %states.1), channel_id=1, replica_groups=mesh['chip'=32,'core'=2,'exp'=12] {'chip','core'}, dimensions={0} | all-to-all | bytes 786432 | tf_op jit(solution)/shard_map/all_to_all | solution.py:311
  56.5 1.9 %scan.1 = bf16[64,16,128]{2,1,0:T(8,128)(2,1)} custom-call(bf16[64,24,128]{2,1,0:T(8,128)(2,1)} %all_to_all.16.in_ref), custom_call_target="tpu_custom_call" | custom-call | flops 524288 | bytes 655360 | tf_op jit(solution)/shard_map/scan/pallas_call | solution.py:312
  58.4 18.3 %all_to_all.17.carried_ref = bf16[64,16,128]{2,1,0:T(8,128)(2,1)} all-to-all(bf16[64,16,128]{2,1,0:T(8,128)(2,1)} %scan.1), channel_id=1, replica_groups=mesh['chip'=32,'core'=2,'exp'=12] {'chip','core'}, dimensions={0} | all-to-all | bytes 524288 | tf_op jit(solution)/shard_map/all_to_all | solution.py:319
  76.7 3.2 %outputs.1 = (bf16[128,512]{1,0:T(8,128)(2,1)}, bf16[128,512]{1,0:T(8,128)(2,1)}, bf16[128,512]{1,0:T(8,128)(2,1)}, bf16[256,256]{1,0:T(8,128)(2,1)}, bf16[80,80]{1,0:T(8,128)(2,1)}) custom-call(bf16[128,512]{1,0:T(8,128)(2,1)} %query_ref.3, bf16[128,512]{1,0:T(8,128)(2,1)} %key_ref.3, bf16[128,512]{1,0:T(8,128)(2,1)} %value_ref.3, ...), custom_call_target="tpu_custom_call" | custom-call | flops 150994944 | bytes 917504 | tf_op jit(solution)/shard_map/outputs/pallas_call | solution.py:324
  79.9 21.6 %all-gather.3.cloned.1.call-done = bf16[768,40,128]{2,1,0:T(8,128)(2,1)} async-done(((bf16[32,40,128]{2,1,0:T(8,128)(2,1)}), bf16[768,40,128]{2,1,0:T(8,128)(2,1)}) %all-gather.3.cloned.1.call-update) | async-done | bytes 7864336 | tf_op jit(solution)/shard_map/all_gather | solution.py:301
  101.5 0.0 copy-done
  101.5 0.0 copy-start.1
  101.5 0.9 copy-done.1
  102.4 0.0 copy-start.2
  102.4 0.7 copy-done.2
  103.1 6.5 %experts.1 = bf16[1,640,256]{2,1,0:T(8,128)(2,1)} custom-call(bf16[2,12,32,40,128]{4,3,2,1,0:T(8,128)(2,1)} %bitcast.6, bf16[256,6144]{1,0:T(8,128)(2,1)S(1)} %bitcast.5, bf16[256,256]{1,0:T(8,128)(2,1)S(1)} %copy-done.1, bf16[80,80]{1,0:T(8,128)(2,1)S(1)} %copy-done.2), custom_call_target="tpu_custom_call" | custom-call | flops 2013265920 | bytes 11010048 | tf_op jit(solution)/shard_map/experts/pallas_call | solution.py:341
Async XLA Ops:
  7.2 94.3 %copy-start = (bf16[1,256,6144]{2,1,0:T(8,128)(2,1)S(1)}, bf16[1,256,6144]{2,1,0:T(8,128)(2,1)}, u32[]{:S(2)}) copy-start(bf16[1,256,6144]{2,1,0:T(8,128)(2,1)} %param.17) | copy-start | bytes 9437188
  7.2 94.3 %all-gather.3.cloned.1.call-start = ((), (), s32[]{:S(2)}) async-start(), calls=%async_computation.3 | async-start | bytes 8192000 | tf_op jit(solution)/shard_map/all_gather | solution.py:301
  101.5 0.9 copy-start.1
  102.4 0.7 copy-start.2
Sparse Core Ops, SparseCore 0:
  29.4 72.0 all-gather.2

commit v4 on v3

--- a/solution.py
+++ b/solution.py
@@ -12,7 +12,6 @@
 LANES = 128
 HEAD = 128
 WHOLE = 8
-TOGETHER = 4
 INTERPRET = False
 
 
@@ -222,56 +221,83 @@
         ).astype(BF16)
 
 
-def expert_kernel(capacity, rows_ref, weight_ref, order_ref, place_ref, out_ref, total):
-    step = pl.program_id(0)
-    cores, places, sources, lines, _ = rows_ref.shape
+def expert_kernel(
+    capacity,
+    turns,
+    rows_hbm,
+    weight_ref,
+    order_hbm,
+    place_hbm,
+    out_ref,
+    rows_ref,
+    order_ref,
+    place_ref,
+    total,
+    arrived,
+    ready,
+):
+    cores, _, sources, lines, _ = rows_ref.shape
     groups = lines // capacity
+    width = groups * LANES
     tail = capacity - WHOLE
     small = sources * groups * tail
     half = sources * capacity
-
-    held = [[rows_ref[c, z] for z in range(places)] for c in range(cores)]
-    rest = [one[:, groups * WHOLE :].reshape(small, LANES) for each in held for one in each]
-    rest = matmul(order_ref[...], jnp.concatenate(rest, axis=1)).astype(BF16)
-    each = small // groups
-    left = []
-    for c in range(cores):
-        whole = [
-            held[c][z][:, f * WHOLE : (f + 1) * WHOLE].reshape(sources * WHOLE, LANES)
-            for z in range(places)
-            for f in range(groups)
-        ]
-        left.append(jnp.concatenate(whole, axis=1))
-        ends = rest[:, c * places * LANES : (c + 1) * places * LANES]
-        ends = [
-            ends[f * each : (f + 1) * each, z * LANES : (z + 1) * LANES]
-            for z in range(places)
-            for f in range(groups)
-        ]
-        left.append(jnp.concatenate(ends, axis=1))
-    product = matmul_t(jnp.concatenate(left, axis=0), weight_ref[...])
-
-    @pl.when(step == 0)
-    def _():
-        total[...] = product
-
-    @pl.when(step > 0)
-    def _():
-        total[...] += product
-
-    @pl.when(step == pl.num_programs(0) - 1)
-    def _():
-        lot = WHOLE // tail
-        size = cores * lot * capacity
-        for g in range(sources // lot):
-            taken = []
-            for c in range(cores):
-                first = c * half + g * lot * WHOLE
-                taken.append(total[first : first + lot * WHOLE])
-                first = c * half + sources * WHOLE + g * lot * tail
-                taken.append(total[first : first + lot * tail])
-            taken = jnp.concatenate(taken, axis=0).astype(BF16)
-            out_ref[0, g * size : (g + 1) * size] = matmul(place_ref[...], taken).astype(BF16)
+    tables = [
+        pltpu.make_async_copy(order_hbm, order_ref, ready.at[0]),
+        pltpu.make_async_copy(place_hbm, place_ref, ready.at[1]),
+    ]
+    copies = [
+        pltpu.make_async_copy(
+            rows_hbm.at[:, first:last], rows_ref.at[:, first:last], arrived.at[i]
+        )
+        for i, (first, last) in enumerate(turns)
+    ]
+    tables[0].start()
+    for copy in copies:
+        copy.start()
+    tables[1].start()
+    tables[0].wait()
+    for i, (first, last) in enumerate(turns):
+        copies[i].wait()
+        count = last - first
+        held = [[rows_ref[c, z] for z in range(first, last)] for c in range(cores)]
+        rest = [one[:, groups * WHOLE :].reshape(small, LANES) for each in held for one in each]
+        rest = matmul(order_ref[...], jnp.concatenate(rest, axis=1)).astype(BF16)
+        each = small // groups
+        left = []
+        for c in range(cores):
+            whole = [
+                held[c][z][:, f * WHOLE : (f + 1) * WHOLE].reshape(sources * WHOLE, LANES)
+                for z in range(count)
+                for f in range(groups)
+            ]
+            left.append(jnp.concatenate(whole, axis=1))
+            ends = rest[:, c * count * LANES : (c + 1) * count * LANES]
+            ends = [
+                ends[f * each : (f + 1) * each, z * LANES : (z + 1) * LANES]
+                for z in range(count)
+                for f in range(groups)
+            ]
+            left.append(jnp.concatenate(ends, axis=1))
+        product = matmul_t(
+            jnp.concatenate(left, axis=0), weight_ref[:, first * width : last * width]
+        )
+        if i == 0:
+            total[...] = product
+        else:
+            total[...] += product
+    tables[1].wait()
+    lot = WHOLE // tail
+    size = cores * lot * capacity
+    for g in range(sources // lot):
+        taken = []
+        for c in range(cores):
+            first = c * half + g * lot * WHOLE
+            taken.append(total[first : first + lot * WHOLE])
+            first = c * half + sources * WHOLE + g * lot * tail
+            taken.append(total[first : first + lot * tail])
+        taken = jnp.concatenate(taken, axis=0).astype(BF16)
+        out_ref[0, g * size : (g + 1) * size] = matmul(place_ref[...], taken).astype(BF16)
 
 
 def per_device(
@@ -337,26 +363,36 @@
 
     places = lax.axis_size("exp")
     rows = 2 * chips * capacity
-    deep = TOGETHER if places % TOGETHER == 0 else 1
+    steps = [places * part // 6 for part in (0, 1, 3, 6)]
+    turns = [(first, last) for first, last in zip(steps, steps[1:]) if last > first]
     hidden_grad = call(
-        functools.partial(expert_kernel, capacity),
+        functools.partial(expert_kernel, capacity, turns),
         jax.ShapeDtypeStruct((1, rows, hidden), BF16),
         2 * rows * width * places * hidden,
         2 * (rows + hidden) * width * places,
-        grid=(places // deep,),
         compiler_params=pltpu.CompilerParams(vmem_limit_bytes=24 << 20),
         in_specs=[
-            pl.BlockSpec((2, deep, chips, lines, LANES), lambda z: (0, z, 0, 0, 0)),
-            pl.BlockSpec((hidden, deep * width), lambda z: (0, z)),
-            pl.BlockSpec((small, small), lambda z: (0, 0)),
-            pl.BlockSpec((size, size), lambda z: (0, 0)),
+            pl.BlockSpec(memory_space=pl.ANY),
+            pl.BlockSpec(memory_space=pltpu.VMEM),
+            pl.BlockSpec(memory_space=pl.ANY),
+            pl.BlockSpec(memory_space=pl.ANY),
         ],
-        out_specs=pl.BlockSpec((1, rows, hidden), lambda z: (0, 0, 0)),
+        out_specs=pl.BlockSpec(memory_space=pltpu.VMEM),
         scratch_shapes=[
+            pltpu.VMEM((2, places, chips, lines, LANES), BF16),
+            pltpu.VMEM((small, small), BF16),
+            pltpu.VMEM((size, size), BF16),
             pltpu.VMEM((rows, hidden), F32),
+            pltpu.SemaphoreType.DMA((len(turns),)),
+            pltpu.SemaphoreType.DMA((2,)),
         ],
         name="experts",
-    )(in_hbm(gathered.reshape(2, places, chips, lines, LANES)), weight, order, place)
+    )(
+        in_hbm(gathered.reshape(2, places, chips, lines, LANES)),
+        weight,
+        in_hbm(order),
+        in_hbm(place),
+    )
     return (query_grad, key_grad, value_grad, hidden_grad)
 
 

time: 117 us -> 116 us (level)
  local copies, waits for them, and re-layouts: 1.64 us -> 0.01 us
    unnamed x6 -> x2, local copies, waits for them, and re-layouts: 1.64 us -> 0.01 us
where the time goes in v4:
time: 116 us; the launch traced here: 115 us
  blocking collectives  63.5 us (55%)
  waiting for transfers between devices  21.6 us (19%)
  Pallas kernels  16.1 us (14%)
  between operations  14.1 us (12%)
    all_to_all x1, blocking collectives, per_device(): spread = lax.all_to_all(states, ('chip', 'core'), 0, 0, tiled=True)  24.8 us
    all_gather x1, waiting for transfers between devices, per_device(): gathered = lax.all_gather(arrived, ('core', 'exp'), axis=0)  21.6 us
    all_to_all x1, blocking collectives, per_device(): arrived = lax.all_to_all(sent, 'chip', 0, 0, tiled=True)  20.4 us
    all_to_all x1, blocking collectives, per_device(): carried = lax.all_to_all(carried, ('chip', 'core'), 0, 0, tiled=True)  18.3 us
    pallas_call x1, Pallas kernels, per_device(): call(functools.partial(expert_kernel, capacity, turns), jax.ShapeDtypeStr...  7.03 us
    pallas_call x1, Pallas kernels, per_device(): call(functools.partial(output_kernel, share, capacity, chips), (flat, fla...  3.17 us
    pallas_call x1, Pallas kernels, per_device(): call(functools.partial(state_kernel, share), jax.ShapeDtypeStruct((blocks...  2.43 us
  transfers between devices with their start and end apart: 1, of which 1 were waited for; matrix products, arithmetic and copies ran while one was open for 0% of the time, Pallas kernels for 6%

profile of v4, /device:TPU:1, one launch (start us, length us, event | category | flops | bytes accessed | tf_op | source)
XLA Modules:
  0.0 115.4 jit_solution(736016456587840306)
XLA Ops:
  7.2 0.0 copy-start
  7.2 0.0 all-gather.3.cloned.1.call-start
  7.2 1.7 %route.1 = bf16[32,40,128]{2,1,0:T(8,128)(2,1)S(1)} custom-call(s32[2,128]{1,0:T(2,128)} %bitcast.9, f32[2,128]{1,0:T(2,128)} %bitcast.10, bf16[128,512]{1,0:T(8,128)(2,1)} %grad_ref.4), custom_call_target="tpu_custom_call" | custom-call | flops 335544320 | bytes 458752 | tf_op jit(solution)/shard_map/route/pallas_call | solution.py:318
  8.9 20.4 %all_to_all.15 = bf16[32,40,128]{2,1,0:T(8,128)(2,1)} all-to-all(bf16[32,40,128]{2,1,0:T(8,128)(2,1)S(1)} %route.1), channel_id=1, replica_groups=mesh['chip'=32,'core'=2,'exp'=12] {'chip'}, dimensions={0} | all-to-all | bytes 655360 | tf_op jit(solution)/shard_map/all_to_all | solution.py:326
  29.3 0.0 all-gather.3.cloned.1.call-update
  29.3 2.4 %states.1 = bf16[64,24,128]{2,1,0:T(8,128)(2,1)} custom-call(bf16[128,512]{1,0:T(8,128)(2,1)} %query_ref.3, bf16[128,512]{1,0:T(8,128)(2,1)} %key_ref.3, bf16[128,512]{1,0:T(8,128)(2,1)} %value_ref.3, bf16[128,512]{1,0:T(8,128)(2,1)} %grad_ref.5, f32[4,128]{1,0:T(4,128)} %bitcast.7), custom_call_target="tpu_custom_call" | custom-call | flops 67108864 | bytes 524288 | tf_op jit(solution)/shard_map/states/pallas_call | solution.py:329
  31.7 24.8 %all_to_all.16.in_ref = bf16[64,24,128]{2,1,0:T(8,128)(2,1)} all-to-all(bf16[64,24,128]{2,1,0:T(8,128)(2,1)} %states.1), channel_id=1, replica_groups=mesh['chip'=32,'core'=2,'exp'=12] {'chip','core'}, dimensions={0} | all-to-all | bytes 786432 | tf_op jit(solution)/shard_map/all_to_all | solution.py:337
  56.5 1.9 %scan.1 = bf16[64,16,128]{2,1,0:T(8,128)(2,1)} custom-call(bf16[64,24,128]{2,1,0:T(8,128)(2,1)} %all_to_all.16.in_ref), custom_call_target="tpu_custom_call" | custom-call | flops 524288 | bytes 655360 | tf_op jit(solution)/shard_map/scan/pallas_call | solution.py:338
  58.4 18.3 %all_to_all.17.carried_ref = bf16[64,16,128]{2,1,0:T(8,128)(2,1)} all-to-all(bf16[64,16,128]{2,1,0:T(8,128)(2,1)} %scan.1), channel_id=1, replica_groups=mesh['chip'=32,'core'=2,'exp'=12] {'chip','core'}, dimensions={0} | all-to-all | bytes 524288 | tf_op jit(solution)/shard_map/all_to_all | solution.py:345
  76.7 3.2 %outputs.1 = (bf16[128,512]{1,0:T(8,128)(2,1)}, bf16[128,512]{1,0:T(8,128)(2,1)}, bf16[128,512]{1,0:T(8,128)(2,1)}, bf16[256,256]{1,0:T(8,128)(2,1)}, bf16[80,80]{1,0:T(8,128)(2,1)}) custom-call(bf16[128,512]{1,0:T(8,128)(2,1)} %query_ref.3, bf16[128,512]{1,0:T(8,128)(2,1)} %key_ref.3, bf16[128,512]{1,0:T(8,128)(2,1)} %value_ref.3, ...), custom_call_target="tpu_custom_call" | custom-call | flops 150994944 | bytes 917504 | tf_op jit(solution)/shard_map/outputs/pallas_call | solution.py:350
  79.9 21.6 %all-gather.3.cloned.1.call-done = bf16[768,40,128]{2,1,0:T(8,128)(2,1)} async-done(((bf16[32,40,128]{2,1,0:T(8,128)(2,1)}), bf16[768,40,128]{2,1,0:T(8,128)(2,1)}) %all-gather.3.cloned.1.call-update) | async-done | bytes 7864336 | tf_op jit(solution)/shard_map/all_gather | solution.py:327
  101.5 0.0 copy-done
  101.5 7.0 %experts.1 = bf16[1,640,256]{2,1,0:T(8,128)(2,1)} custom-call(bf16[2,12,32,40,128]{4,3,2,1,0:T(8,128)(2,1)} %bitcast.6, bf16[256,6144]{1,0:T(8,128)(2,1)S(1)} %bitcast.5, bf16[256,256]{1,0:T(8,128)(2,1)} %get-tuple-element.18.order_hbm, bf16[80,80]{1,0:T(8,128)(2,1)} %get-tuple-element.19.place_hbm), custom_call_target="tpu_custom_call" | custom-call | flops 2013265920 | bytes 11010048 | tf_op jit(solution)/shard_map/experts/pallas_call | solution.py:368
Async XLA Ops:
  7.2 94.3 %copy-start = (bf16[1,256,6144]{2,1,0:T(8,128)(2,1)S(1)}, bf16[1,256,6144]{2,1,0:T(8,128)(2,1)}, u32[]{:S(2)}) copy-start(bf16[1,256,6144]{2,1,0:T(8,128)(2,1)} %param.17) | copy-start | bytes 9437188
  7.2 94.3 %all-gather.3.cloned.1.call-start = ((), (), s32[]{:S(2)}) async-start(), calls=%async_computation.3 | async-start | bytes 8192000 | tf_op jit(solution)/shard_map/all_gather | solution.py:327
Sparse Core Ops, SparseCore 0:
  29.4 72.0 all-gather.2

commit v5 on v3

--- a/solution.py
+++ b/solution.py
@@ -150,9 +150,9 @@
     behind = jnp.zeros((share, LANES), F32)
     for b in range(blocks):
         now, ahead = step(ahead, b, 0)
-        out_ref[b, 0:share] = now.astype(BF16)
+        out_ref[b, 0:share] = now
         now, behind = step(behind, blocks - 1 - b, share)
-        out_ref[blocks - 1 - b, share : 2 * share] = now.astype(BF16)
+        out_ref[blocks - 1 - b, share : 2 * share] = now
 
 
 def fill_tables(capacity, sources, groups, order_ref, place_ref):
@@ -201,8 +201,8 @@
         since = as_column(since_row, eye)
         closing = since_row[:, length - 1 : length]
         carried = carried_ref[h * per_head : (h + 1) * per_head]
-        leading = carried[:, 0:share].reshape(HEAD, LANES)
-        trailing = carried[:, share : 2 * share].reshape(HEAD, LANES)
+        leading = pieces(carried[:, 0:share].reshape(HEAD, LANES))
+        trailing = pieces(carried[:, share : 2 * share].reshape(HEAD, LANES))
         q, k, v, g = (ref[:, lanes] for ref in (query_ref, key_ref, value_ref, grad_ref))
         weights = jnp.where(row >= col, jnp.exp(jnp.where(row >= col, since - since_row, 0.0)), 0.0)
         turned = jnp.where(row <= col, jnp.exp(jnp.where(row <= col, since_row - since, 0.0)), 0.0)
@@ -211,14 +211,14 @@
         grad_scores_t = (matmul_t(v, g) * turned).astype(BF16)
         scores_t = (matmul_t(k, q) * turned).astype(BF16)
         dq_ref[:, lanes] = (
-            matmul(grad_scores, k) + jnp.exp(since) * matmul_t(g, leading)
+            matmul(grad_scores, k) + jnp.exp(since) * (matmul_t(g, leading[0]) + matmul_t(g, leading[1]))
         ).astype(BF16)
         dk_ref[:, lanes] = (
             matmul(grad_scores_t, q)
-            + until * matmul_t(v, trailing)
+            + until * (matmul_t(v, trailing[0]) + matmul_t(v, trailing[1]))
         ).astype(BF16)
         dv_ref[:, lanes] = (
-            matmul(scores_t, g) + until * matmul(k, trailing)
+            matmul(scores_t, g) + until * (matmul(k, trailing[0]) + matmul(k, trailing[1]))
         ).astype(BF16)
 
 
@@ -249,7 +249,9 @@
             for f in range(groups)
         ]
         left.append(jnp.concatenate(ends, axis=1))
-    product = matmul_t(jnp.concatenate(left, axis=0), weight_ref[...])
+    deep = places * groups * LANES
+    weight = weight_ref[:, pl.ds(pl.multiple_of(step * deep, deep), deep)]
+    product = matmul_t(jnp.concatenate(left, axis=0), weight)
 
     @pl.when(step == 0)
     def _():
@@ -311,7 +313,7 @@
     spread = lax.all_to_all(states, ("chip", "core"), 0, 0, tiled=True)
     carried = call(
         functools.partial(scan_kernel, share),
-        jax.ShapeDtypeStruct((blocks, 2 * share, LANES), BF16),
+        jax.ShapeDtypeStruct((blocks, 2 * share, LANES), F32),
         8 * blocks * share * LANES,
         10 * blocks * share * LANES,
         name="scan",
@@ -347,7 +349,7 @@
         compiler_params=pltpu.CompilerParams(vmem_limit_bytes=24 << 20),
         in_specs=[
             pl.BlockSpec((2, deep, chips, lines, LANES), lambda z: (0, z, 0, 0, 0)),
-            pl.BlockSpec((hidden, deep * width), lambda z: (0, z)),
+            pl.BlockSpec(memory_space=pltpu.VMEM),
             pl.BlockSpec((small, small), lambda z: (0, 0)),
             pl.BlockSpec((size, size), lambda z: (0, 0)),
         ],
@@ -356,7 +358,7 @@
             pltpu.VMEM((rows, hidden), F32),
         ],
         name="experts",
-    )(in_hbm(gathered.reshape(2, places, chips, lines, LANES)), weight, order, place)
+    )(in_hbm(gathered.reshape(2, places, chips, lines, LANES)), weight, in_hbm(order), in_hbm(place))
     return (query_grad, key_grad, value_grad, hidden_grad)
 
 

time: 117 us -> 115 us (0.983)
  waiting for transfers between devices: 21.7 us -> 15.9 us
  blocking collectives: 63.5 us -> 68.8 us
  local copies, waits for them, and re-layouts: 1.64 us -> 0.01 us
    all_gather x1, waiting for transfers between devices: 21.6 us -> 15.9 us  [per_device(): gathered = lax.all_gather(arrived, ('core', 'exp'), axis=0)]
    all_to_all x1, blocking collectives: 18.3 us -> 23.6 us  [per_device(): carried = lax.all_to_all(carried, ('chip', 'core'), 0, 0, tiled=True)]
    unnamed x6 -> x2, local copies, waits for them, and re-layouts: 1.64 us -> 0.01 us
  transfers between devices with their start and end apart: 1 -> 1, of which waited for: 1 -> 1; matrix products, arithmetic and copies ran while one was open for 0% -> 0% of each run, Pallas kernels for 6% -> 7%
where the time goes in v5:
time: 115 us
  blocking collectives  68.8 us (60%)
  Pallas kernels  16.1 us (14%)
  waiting for transfers between devices  15.9 us (14%)
  between operations  14 us (12%)
    all_to_all x1, blocking collectives, per_device(): spread = lax.all_to_all(states, ('chip', 'core'), 0, 0, tiled=True)  24.8 us
    all_to_all x1, blocking collectives, per_device(): carried = lax.all_to_all(carried, ('chip', 'core'), 0, 0, tiled=True)  23.6 us
    all_to_all x1, blocking collectives, per_device(): arrived = lax.all_to_all(sent, 'chip', 0, 0, tiled=True)  20.4 us
    all_gather x1, waiting for transfers between devices, per_device(): gathered = lax.all_gather(arrived, ('core', 'exp'), axis=0)  15.9 us
    pallas_call x1, Pallas kernels, per_device(): call(functools.partial(expert_kernel, capacity), jax.ShapeDtypeStruct((1,...  6.52 us
    pallas_call x1, Pallas kernels, per_device(): call(functools.partial(output_kernel, share, capacity, chips), (flat, fla...  3.46 us
    pallas_call x1, Pallas kernels, per_device(): call(functools.partial(state_kernel, share), jax.ShapeDtypeStruct((blocks...  2.44 us
  transfers between devices with their start and end apart: 1, of which 1 were waited for; matrix products, arithmetic and copies ran while one was open for 0% of the time, Pallas kernels for 7%

profile of v5, /device:TPU:1, one launch (start us, length us, event | category | flops | bytes accessed | tf_op | source)
XLA Modules:
  0.0 114.9 jit_solution(5316993377169860665)
XLA Ops:
  7.2 0.0 copy-start
  7.2 0.0 all-gather.3.cloned.1.call-start
  7.2 1.7 %route.1 = bf16[32,40,128]{2,1,0:T(8,128)(2,1)S(1)} custom-call(s32[2,128]{1,0:T(2,128)} %bitcast.9, f32[2,128]{1,0:T(2,128)} %bitcast.10, bf16[128,512]{1,0:T(8,128)(2,1)} %grad_ref.4), custom_call_target="tpu_custom_call" | custom-call | flops 335544320 | bytes 458752 | tf_op jit(solution)/shard_map/route/pallas_call | solution.py:294
  8.9 20.4 %all_to_all.15 = bf16[32,40,128]{2,1,0:T(8,128)(2,1)} all-to-all(bf16[32,40,128]{2,1,0:T(8,128)(2,1)S(1)} %route.1), channel_id=1, replica_groups=mesh['chip'=32,'core'=2,'exp'=12] {'chip'}, dimensions={0} | all-to-all | bytes 655360 | tf_op jit(solution)/shard_map/all_to_all | solution.py:302
  29.3 0.0 all-gather.3.cloned.1.call-update
  29.3 2.4 %states.1 = bf16[64,24,128]{2,1,0:T(8,128)(2,1)} custom-call(bf16[128,512]{1,0:T(8,128)(2,1)} %query_ref.3, bf16[128,512]{1,0:T(8,128)(2,1)} %key_ref.3, bf16[128,512]{1,0:T(8,128)(2,1)} %value_ref.3, bf16[128,512]{1,0:T(8,128)(2,1)} %grad_ref.5, f32[4,128]{1,0:T(4,128)} %bitcast.7), custom_call_target="tpu_custom_call" | custom-call | flops 67108864 | bytes 524288 | tf_op jit(solution)/shard_map/states/pallas_call | solution.py:305
  31.8 24.8 %all_to_all.16.in_ref = bf16[64,24,128]{2,1,0:T(8,128)(2,1)} all-to-all(bf16[64,24,128]{2,1,0:T(8,128)(2,1)} %states.1), channel_id=1, replica_groups=mesh['chip'=32,'core'=2,'exp'=12] {'chip','core'}, dimensions={0} | all-to-all | bytes 786432 | tf_op jit(solution)/shard_map/all_to_all | solution.py:313
  56.5 2.0 %scan.1 = f32[64,16,128]{2,1,0:T(8,128)} custom-call(bf16[64,24,128]{2,1,0:T(8,128)(2,1)} %all_to_all.16.in_ref), custom_call_target="tpu_custom_call" | custom-call | flops 524288 | bytes 655360 | tf_op jit(solution)/shard_map/scan/pallas_call | solution.py:314
  58.5 23.6 %all_to_all.17.carried_ref = f32[64,16,128]{2,1,0:T(8,128)} all-to-all(f32[64,16,128]{2,1,0:T(8,128)} %scan.1), channel_id=1, replica_groups=mesh['chip'=32,'core'=2,'exp'=12] {'chip','core'}, dimensions={0} | all-to-all | bytes 1048576 | tf_op jit(solution)/shard_map/all_to_all | solution.py:321
  82.2 3.5 %outputs.1 = (bf16[128,512]{1,0:T(8,128)(2,1)}, bf16[128,512]{1,0:T(8,128)(2,1)}, bf16[128,512]{1,0:T(8,128)(2,1)}, bf16[256,256]{1,0:T(8,128)(2,1)}, bf16[80,80]{1,0:T(8,128)(2,1)}) custom-call(bf16[128,512]{1,0:T(8,128)(2,1)} %query_ref.3, bf16[128,512]{1,0:T(8,128)(2,1)} %key_ref.3, bf16[128,512]{1,0:T(8,128)(2,1)} %value_ref.3, ...), custom_call_target="tpu_custom_call" | custom-call | flops 150994944 | bytes 917504 | tf_op jit(solution)/shard_map/outputs/pallas_call | solution.py:326
  85.6 15.9 %all-gather.3.cloned.1.call-done = bf16[768,40,128]{2,1,0:T(8,128)(2,1)} async-done(((bf16[32,40,128]{2,1,0:T(8,128)(2,1)}), bf16[768,40,128]{2,1,0:T(8,128)(2,1)}) %all-gather.3.cloned.1.call-update) | async-done | bytes 7864336 | tf_op jit(solution)/shard_map/all_gather | solution.py:303
  101.5 0.0 copy-done
  101.5 6.5 %experts.1 = bf16[1,640,256]{2,1,0:T(8,128)(2,1)} custom-call(bf16[2,12,32,40,128]{4,3,2,1,0:T(8,128)(2,1)} %bitcast.6, bf16[256,6144]{1,0:T(8,128)(2,1)S(1)} %bitcast.5, bf16[256,256]{1,0:T(8,128)(2,1)} %get-tuple-element.18.order_ref, bf16[80,80]{1,0:T(8,128)(2,1)} %get-tuple-element.19.place_ref), custom_call_target="tpu_custom_call" | custom-call | flops 2013265920 | bytes 11010048 | tf_op jit(solution)/shard_map/experts/pallas_call | solution.py:343
Async XLA Ops:
  7.2 94.3 %copy-start = (bf16[1,256,6144]{2,1,0:T(8,128)(2,1)S(1)}, bf16[1,256,6144]{2,1,0:T(8,128)(2,1)}, u32[]{:S(2)}) copy-start(bf16[1,256,6144]{2,1,0:T(8,128)(2,1)} %param.17) | copy-start | bytes 9437188
  7.2 94.3 %all-gather.3.cloned.1.call-start = ((), (), s32[]{:S(2)}) async-start(), calls=%async_computation.3 | async-start | bytes 8192000 | tf_op jit(solution)/shard_map/all_gather | solution.py:303
Sparse Core Ops, SparseCore 0:
  29.4 72.0 all-gather.2

commit v6 on v5

--- a/solution.py
+++ b/solution.py
@@ -12,7 +12,7 @@
 LANES = 128
 HEAD = 128
 WHOLE = 8
-TOGETHER = 4
+TOGETHER = 6
 INTERPRET = False
 
 

time: 115 us -> 115 us (level)
  no operation moved by 1% of the time
where the time goes in v6:
time: 115 us; the launch traced here: 114 us
  blocking collectives  68.8 us (60%)
  waiting for transfers between devices  15.9 us (14%)
  Pallas kernels  15.5 us (13%)
  between operations  14 us (12%)
    all_to_all x1, blocking collectives, per_device(): spread = lax.all_to_all(states, ('chip', 'core'), 0, 0, tiled=True)  24.8 us
    all_to_all x1, blocking collectives, per_device(): carried = lax.all_to_all(carried, ('chip', 'core'), 0, 0, tiled=True)  23.6 us
    all_to_all x1, blocking collectives, per_device(): arrived = lax.all_to_all(sent, 'chip', 0, 0, tiled=True)  20.4 us
    all_gather x1, waiting for transfers between devices, per_device(): gathered = lax.all_gather(arrived, ('core', 'exp'), axis=0)  15.9 us
    pallas_call x1, Pallas kernels, per_device(): call(functools.partial(expert_kernel, capacity), jax.ShapeDtypeStruct((1,...  5.96 us
    pallas_call x1, Pallas kernels, per_device(): call(functools.partial(output_kernel, share, capacity, chips), (flat, fla...  3.46 us
    pallas_call x1, Pallas kernels, per_device(): call(functools.partial(state_kernel, share), jax.ShapeDtypeStruct((blocks...  2.44 us
  transfers between devices with their start and end apart: 1, of which 1 were waited for; matrix products, arithmetic and copies ran while one was open for 0% of the time, Pallas kernels for 7%

profile of v6, /device:TPU:1, one launch (start us, length us, event | category | flops | bytes accessed | tf_op | source)
XLA Modules:
  0.0 114.3 jit_solution(13125742888561173672)
XLA Ops:
  7.2 0.0 copy-start
  7.2 0.0 all-gather.3.cloned.1.call-start
  7.2 1.7 %route.1 = bf16[32,40,128]{2,1,0:T(8,128)(2,1)S(1)} custom-call(s32[2,128]{1,0:T(2,128)} %bitcast.9, f32[2,128]{1,0:T(2,128)} %bitcast.10, bf16[128,512]{1,0:T(8,128)(2,1)} %grad_ref.4), custom_call_target="tpu_custom_call" | custom-call | flops 335544320 | bytes 458752 | tf_op jit(solution)/shard_map/route/pallas_call | solution.py:294
  8.9 20.4 %all_to_all.15 = bf16[32,40,128]{2,1,0:T(8,128)(2,1)} all-to-all(bf16[32,40,128]{2,1,0:T(8,128)(2,1)S(1)} %route.1), channel_id=1, replica_groups=mesh['chip'=32,'core'=2,'exp'=12] {'chip'}, dimensions={0} | all-to-all | bytes 655360 | tf_op jit(solution)/shard_map/all_to_all | solution.py:302
  29.3 0.0 all-gather.3.cloned.1.call-update
  29.3 2.4 %states.1 = bf16[64,24,128]{2,1,0:T(8,128)(2,1)} custom-call(bf16[128,512]{1,0:T(8,128)(2,1)} %query_ref.3, bf16[128,512]{1,0:T(8,128)(2,1)} %key_ref.3, bf16[128,512]{1,0:T(8,128)(2,1)} %value_ref.3, bf16[128,512]{1,0:T(8,128)(2,1)} %grad_ref.5, f32[4,128]{1,0:T(4,128)} %bitcast.7), custom_call_target="tpu_custom_call" | custom-call | flops 67108864 | bytes 524288 | tf_op jit(solution)/shard_map/states/pallas_call | solution.py:305
  31.8 24.8 %all_to_all.16.in_ref = bf16[64,24,128]{2,1,0:T(8,128)(2,1)} all-to-all(bf16[64,24,128]{2,1,0:T(8,128)(2,1)} %states.1), channel_id=1, replica_groups=mesh['chip'=32,'core'=2,'exp'=12] {'chip','core'}, dimensions={0} | all-to-all | bytes 786432 | tf_op jit(solution)/shard_map/all_to_all | solution.py:313
  56.5 2.0 %scan.1 = f32[64,16,128]{2,1,0:T(8,128)} custom-call(bf16[64,24,128]{2,1,0:T(8,128)(2,1)} %all_to_all.16.in_ref), custom_call_target="tpu_custom_call" | custom-call | flops 524288 | bytes 655360 | tf_op jit(solution)/shard_map/scan/pallas_call | solution.py:314
  58.5 23.6 %all_to_all.17.carried_ref = f32[64,16,128]{2,1,0:T(8,128)} all-to-all(f32[64,16,128]{2,1,0:T(8,128)} %scan.1), channel_id=1, replica_groups=mesh['chip'=32,'core'=2,'exp'=12] {'chip','core'}, dimensions={0} | all-to-all | bytes 1048576 | tf_op jit(solution)/shard_map/all_to_all | solution.py:321
  82.2 3.5 %outputs.1 = (bf16[128,512]{1,0:T(8,128)(2,1)}, bf16[128,512]{1,0:T(8,128)(2,1)}, bf16[128,512]{1,0:T(8,128)(2,1)}, bf16[256,256]{1,0:T(8,128)(2,1)}, bf16[80,80]{1,0:T(8,128)(2,1)}) custom-call(bf16[128,512]{1,0:T(8,128)(2,1)} %query_ref.3, bf16[128,512]{1,0:T(8,128)(2,1)} %key_ref.3, bf16[128,512]{1,0:T(8,128)(2,1)} %value_ref.3, ...), custom_call_target="tpu_custom_call" | custom-call | flops 150994944 | bytes 917504 | tf_op jit(solution)/shard_map/outputs/pallas_call | solution.py:326
  85.6 15.9 %all-gather.3.cloned.1.call-done = bf16[768,40,128]{2,1,0:T(8,128)(2,1)} async-done(((bf16[32,40,128]{2,1,0:T(8,128)(2,1)}), bf16[768,40,128]{2,1,0:T(8,128)(2,1)}) %all-gather.3.cloned.1.call-update) | async-done | bytes 7864336 | tf_op jit(solution)/shard_map/all_gather | solution.py:303
  101.5 0.0 copy-done
  101.5 6.0 %experts.1 = bf16[1,640,256]{2,1,0:T(8,128)(2,1)} custom-call(bf16[2,12,32,40,128]{4,3,2,1,0:T(8,128)(2,1)} %bitcast.6, bf16[256,6144]{1,0:T(8,128)(2,1)S(1)} %bitcast.5, bf16[256,256]{1,0:T(8,128)(2,1)} %get-tuple-element.18.order_ref, bf16[80,80]{1,0:T(8,128)(2,1)} %get-tuple-element.19.place_ref), custom_call_target="tpu_custom_call" | custom-call | flops 2013265920 | bytes 11010048 | tf_op jit(solution)/shard_map/experts/pallas_call | solution.py:343
Async XLA Ops:
  7.2 94.3 %copy-start = (bf16[1,256,6144]{2,1,0:T(8,128)(2,1)S(1)}, bf16[1,256,6144]{2,1,0:T(8,128)(2,1)}, u32[]{:S(2)}) copy-start(bf16[1,256,6144]{2,1,0:T(8,128)(2,1)} %param.17) | copy-start | bytes 9437188
  7.2 94.3 %all-gather.3.cloned.1.call-start = ((), (), s32[]{:S(2)}) async-start(), calls=%async_computation.3 | async-start | bytes 8192000 | tf_op jit(solution)/shard_map/all_gather | solution.py:303
Sparse Core Ops, SparseCore 0:
  29.4 72.0 all-gather.2
